TPU v7x, 32 devices: a whole 2x2x4 slice. The times are simulated.
32 devices in a mesh: groups: 2 (over x), pb: 16 (over z, y, core).
Axes of the slice: x: 2, y: 2, z: 4, core: 2. Of those that a mesh axis runs over, the one named last changes fastest.
Arguments:
- frames: float32 [64, 512, 2048], P(('groups', 'pb')), parts along dimension 0, as said below
- valid_mask: int32 [64], P(('groups', 'pb')), parts along dimension 0, may hold values from 0 to 1, as said below
Outputs:
- correlations: float32 [128, 512, 512], P('groups', 'pb'), parts along dimension 0
There are 2 independent parts, one for each index of `groups`. A program takes and returns all parts, laid end to end along the dimension named above; each array names one. Nothing has to cross between parts.
Inputs may be any that keep to these rules, and one draw needn't show every extreme that they name: `valid_mask`: the window holds at least one valid shot; the aligned blocks of 2 shots (the shots of one index of pb) may differ in their rate of valid shots. `frames`: frames share an anisotropic pattern across shots beside independent fluctuations.
All inputs are finite; a program needn't handle non-finite values.
Results may differ from a plain program's by a relative error of at most 0.02.
Values may be sent and summed in bfloat16 or wider, within the bound.
No kernel may reach another device: no remote copies, remote signals or barrier semaphores. Data moves between devices by JAX's collectives and lax.ppermute only.
A program may use at most 128 MiB of HBM per device.

v0:
```python
import math

import jax
import jax.numpy as jnp
from jax import lax
from jax.sharding import PartitionSpec as P

HARMONICS = 64


def angle_table(angles, harmonics):
    harmonic_order = 2 * (jnp.arange(harmonics, dtype=jnp.int32) + 1)
    angle_index = jnp.arange(angles, dtype=jnp.int32)
    wrapped = angle_index[:, None] * harmonic_order[None, :] % angles
    phase_angle = wrapped.astype(jnp.float32) * (2.0 * math.pi / angles)
    scale_factor = 1.0 / math.sqrt(angles)
    return jnp.concatenate([jnp.cos(phase_angle), -jnp.sin(phase_angle)], axis=1) * scale_factor


def cross_block(block_left, block_right):
    shot_rows, left_cycles, doubled = block_left.shape
    right_cycles = block_right.shape[1]
    half_width = doubled // 2
    split_left = block_left.reshape(shot_rows, left_cycles, 2, half_width)
    split_right = block_right.reshape(shot_rows, right_cycles, 2, half_width)
    return jnp.einsum("sqcn,spcn->nqp", split_left, split_right, preferred_element_type=jnp.float32)


def body(frames, valid_mask):
    shot_dev, cycles, angles = frames.shape
    harmonics = HARMONICS
    phase_table = angle_table(angles, harmonics)
    weights = valid_mask.astype(jnp.float32)
    projected = jnp.dot(
        frames.reshape(shot_dev * cycles, angles), phase_table, precision=lax.Precision.HIGHEST
    )
    spectra = (weights[:, None, None] * projected.reshape(shot_dev, cycles, 2 * harmonics)).astype(
        jnp.bfloat16
    )
    valid_total, sum_spectra = lax.psum(
        (jnp.sum(weights), jnp.sum(spectra.astype(jnp.float32), axis=0)), "pb"
    )
    axis_size = lax.axis_size("pb")
    cycle_width = cycles // axis_size
    my_index = lax.axis_index("pb")
    cycle_start = my_index * cycle_width
    piece = lax.all_gather(spectra, "pb", axis=0, tiled=True)
    own_cycles = lax.dynamic_slice_in_dim(piece, cycle_start, cycle_width, 1)
    panel = cross_block(own_cycles, piece)
    mean_cycles = sum_spectra / valid_total
    mean_own = lax.dynamic_slice_in_dim(mean_cycles, cycle_start, cycle_width, 0)
    outer_mean = jnp.einsum(
        "qcn,pcn->nqp",
        mean_own.reshape(cycle_width, 2, harmonics),
        mean_cycles.reshape(cycles, 2, harmonics),
        precision=lax.Precision.HIGHEST,
    )
    return panel / valid_total - outer_mean


def solution(mesh):
    placed = (P(("groups", "pb"), None, None), P(("groups", "pb")))
    return jax.shard_map(
        body, mesh=mesh, in_specs=placed, out_specs=P("groups", "pb", None), check_vma=False
    )
```

profile of v0, /device:TPU:0, one launch (start us, length us, event | category | flops | bytes accessed | tf_op | source)
XLA Modules:
  0.0 197.6 jit_solution(10584868969886470733)
XLA Ops:
  6.5 0.0 all-reduce.2.cloned.1.call-start
  6.5 4.1 %fusion.12 = (f32[2048,64]{1,0:T(8,128)S(1)}, f32[2048,64]{1,0:T(8,128)S(1)}) fusion(s32[64]{0:T(128)S(1)} %add_multiply_fusion), kind=kLoop, calls=%fused_computation.21 | loop fusion | flops 1966080 | bytes 1048832 | tf_op jit(solution)/shard_map/cos | solution.py:17
  10.7 0.0 copy-start
  10.7 10.2 %convolution_bitcast_fusion = f32[1024,128]{0,1:T(8,128)S(1)} fusion(f32[1024,2048]{1,0:T(8,128)} %bitcast.15, f32[2048,64]{1,0:T(8,128)S(1)} %get-tuple-element.8, f32[2048,64]{1,0:T(8,128)S(1)} %get-tuple-element.7), kind=kOutput, calls=%fused_computation.7 | convolution fusion | flops 3221749760 | bytes 9961472 | tf_op jit(solution)/shard_map/dot_general | solution.py:34
  20.9 0.2 copy.25
  21.1 0.0 copy-done
  21.1 1.5 convert_reduce_fusion
  22.7 0.0 all-reduce.2.cloned.1.call-update
  22.7 0.0 all-gather.2.cloned.1.call-start
  22.7 0.7 all-gather.2.cloned.1.call-update
  23.4 0.6 convert_reduce_fusion.1
  24.0 35.7 %psum.14 = f32[]{:T(128)} all-reduce(f32[]{:T(128)} %convert_reduce_fusion.1), channel_id=1, replica_groups=mesh['groups'=2,'pb'=16] {'pb'}, use_global_device_ids=true, to_apply=%region_1.2 | all-reduce | flops 1 | bytes 8 | tf_op jit(solution)/shard_map/psum | solution.py:40
  59.8 55.6 %all-reduce.2.cloned.1.call-done = f32[512,128]{1,0:T(8,128)} async-done(((f32[512,128]{1,0:T(8,128)}), f32[512,128]{1,0:T(8,128)}) %all-reduce.2.cloned.1.call-update) | async-done | bytes 262160 | tf_op jit(solution)/shard_map/psum | solution.py:40
  115.3 1.5 broadcast_divide_fusion
  116.9 0.1 copy.21
  117.0 0.1 reshape.28
  117.1 0.1 copy.22
  117.2 51.2 %all-gather.2.cloned.1.call-done = bf16[32,512,128]{2,1,0:T(8,128)(2,1)} async-done(((bf16[2,512,128]{2,1,0:T(8,128)(2,1)}), bf16[32,512,128]{2,1,0:T(8,128)(2,1)}) %all-gather.2.cloned.1.call-update) | async-done | bytes 4194320 | tf_op jit(solution)/shard_map/all_gather | solution.py:47
  168.4 1.0 constant_dynamic-slice_fusion.1
  169.4 0.2 reshape.26
  169.6 1.8 copy.19
  171.4 6.4 %copy.18 = bf16[32,512,128]{1,2,0:T(8,128)(2,1)} copy(bf16[32,512,128]{2,1,0:T(8,128)(2,1)} %all-gather.2.cloned.1.call-done) | data formatting | bytes 8388608 | tf_op jit(solution)/shard_map/all_gather | solution.py:47
  177.8 7.1 %fusion.1 = f32[64,32,512,1]{2,1,3,0:T(8,128)S(1)} fusion(bf16[32,32,2,64]{0,1,2,3:T(8,128)(2,1)S(1)} %copy.19, bf16[32,512,2,64]{1,3,2,0:T(8,128)(2,1)} %bitcast.14), kind=kOutput, calls=%fused_computation.2 | convolution fusion | flops 134217728 | bytes 8650752 | tf_op jit(solution)/shard_map/sqcn,spcn->nqp/dot_general | solution.py:26
  184.9 5.9 %fusion = f32[64,32,512]{2,1,0:T(8,128)} fusion(f32[64,32,512,1]{2,1,3,0:T(8,128)S(1)} %fusion.1, f32[32,2,64]{0,1,2:T(2,128)S(1)} %copy.22, f32[]{:T(128)} %psum.14, f32[512,2,64]{0,2,1:T(8,128)S(1)} %bitcast.17), kind=kOutput, calls=%fused_computation.1 | convolution fusion | flops 27262976 | bytes 8667140 | tf_op jit(solution)/shard_map/qcn,pcn->nqp/dot_general | solution.py:52
  (3 shorter events, 0.0 us)
Async XLA Ops:
  6.5 108.8 %all-reduce.2.cloned.1.call-start = ((), (), s32[]{:S(2)}) async-start(), calls=%async_computation.1 | async-start | bytes 524288 | tf_op jit(solution)/shard_map/psum | solution.py:40
  10.7 10.4 %copy-start = (s32[2]{0:T(128)S(1)}, s32[2]{0:T(128)}, u32[]{:S(2)}) copy-start(s32[2]{0:T(128)} %param.3) | copy-start | bytes 28
  22.7 145.7 %all-gather.2.cloned.1.call-start = ((), (), s32[]{:S(2)}) async-start(), calls=%async_computation | async-start | bytes 4456448 | tf_op jit(solution)/shard_map/all_gather | solution.py:47
Sparse Core Ops, SparseCore 0:
  22.8 92.4 all-reduce.1
  117.5 50.8 all-gather.1
where the time goes:
time: 198 us
  waiting for transfers between devices  107 us (54%)
  blocking collectives  35.7 us (18%)
  matrix products  23.2 us (12%)
  between operations  13.5 us (7%)
  local copies, waits for them, and re-layouts  9.92 us (5%)
  other arithmetic  7.76 us (4%)
    psum x1, waiting for transfers between devices, body(): lax.psum((jnp.sum(weights), jnp.sum(spectra.astype(jnp.float32), axis=0))...  55.6 us
    all_gather x1, waiting for transfers between devices, body(): piece = lax.all_gather(spectra, 'pb', axis=0, tiled=True)  51.2 us
    psum x1, blocking collectives, body(): lax.psum((jnp.sum(weights), jnp.sum(spectra.astype(jnp.float32), axis=0))...  35.7 us
    dot_general x1, matrix products, body(): jnp.dot(frames.reshape(shot_dev * cycles, angles), phase_table, precision...  10.2 us
    dot_general x1, matrix products, cross_block(): jnp.einsum('sqcn,spcn->nqp', split_left, split_right, preferred_element_t...  7.11 us
    all_gather x1, local copies, waits for them, and re-layouts, body(): piece = lax.all_gather(spectra, 'pb', axis=0, tiled=True)  6.43 us
    dot_general x1, matrix products, body(): jnp.einsum('qcn,pcn->nqp', mean_own.reshape(cycle_width, 2, harmonics), m...  5.88 us
    cos x1, other arithmetic, angle_table(): jnp.cos(phase_angle)  4.13 us
  transfers between devices with their start and end apart: 2, of which 2 were waited for; matrix products, arithmetic and copies ran while one was open for 1% of the time, Pallas kernels for 0%

commit v1 on v0

v1 whole, which is shorter than its diff:
```python
import functools
import math

import jax
import jax.numpy as jnp
import numpy as np
from jax import lax
from jax.experimental import pallas as pl
from jax.experimental.pallas import tpu as pltpu
from jax.sharding import PartitionSpec as P

HARMONICS = 64
LANES = 128
GROUP = 4
ROWS = 4 * GROUP
CHUNKS = 2


def half_table(angles):
    order = 2 * (np.arange(HARMONICS) + 1)
    wrapped = np.arange(angles // 2)[:, None] * order[None, :] % angles
    phase = wrapped * (2.0 * math.pi / angles)
    table = np.stack([np.cos(phase), -np.sin(phase)], axis=-1).reshape(angles // 2, 2 * HARMONICS)
    table = (2.0 / math.sqrt(angles)) * table
    high = table.astype(jnp.bfloat16)
    low = (table - high.astype(np.float64)).astype(jnp.bfloat16)
    return np.concatenate([high, low], axis=1)


def spectra_kernel(mask_ref, frames_ref, table_ref, *refs):
    out_refs = refs[:CHUNKS]
    buf, table, sems = refs[CHUNKS:]
    shots, cycles, angles = frames_ref.shape
    blocks = cycles // LANES
    half = angles // 2
    groups = HARMONICS // GROUP // CHUNKS
    copies = [pltpu.make_async_copy(table_ref, table, sems.at[shots * blocks])]
    for q in range(blocks):
        for s in range(shots):
            copies.append(
                pltpu.make_async_copy(
                    frames_ref.at[s, pl.ds(q * LANES, LANES), :], buf.at[q * shots + s], sems.at[q * shots + s]
                )
            )
    for copy in copies:
        copy.start()
    weights = [mask_ref[s].astype(jnp.float32) for s in range(shots)]
    row = lax.broadcasted_iota(jnp.int32, (ROWS, LANES), 0)
    tile = jnp.where(row < ROWS // 2, weights[0], weights[1]).astype(jnp.bfloat16)
    out_refs[0][pl.ds(groups * blocks * ROWS, ROWS), :] = tile
    copies[0].wait()
    for q in range(blocks):
        turned = []
        for s in range(shots):
            copies[1 + q * shots + s].wait()
            scale = 0.5 * weights[s]
            x = buf[q * shots + s]
            folded = x[:, :half] * scale + x[:, half:] * scale
            high = folded.astype(jnp.bfloat16)
            low = (folded - high.astype(jnp.float32)).astype(jnp.bfloat16)
            pair = jnp.dot(high, table[...], preferred_element_type=jnp.float32)
            pair += jnp.dot(low, table[...], preferred_element_type=jnp.float32)
            turned.append((pair[:, :LANES] + pair[:, LANES:]).T)
        for g in range(HARMONICS // GROUP):
            part = slice(g * 2 * GROUP, (g + 1) * 2 * GROUP)
            block = jnp.concatenate([turned[0][part], turned[1][part]], axis=0).astype(jnp.bfloat16)
            out_refs[g // groups][pl.ds((g % groups * blocks + q) * ROWS, ROWS), :] = block


def spectra_call(frames, valid_mask):
    shots, cycles, angles = frames.shape
    blocks = cycles // LANES
    groups = HARMONICS // GROUP // CHUNKS
    rows = [groups * blocks * ROWS + (ROWS if c == 0 else 0) for c in range(CHUNKS)]
    table = jnp.asarray(half_table(angles))
    return pl.pallas_call(
        spectra_kernel,
        out_shape=[jax.ShapeDtypeStruct((r, LANES), jnp.bfloat16) for r in rows],
        in_specs=[
            pl.BlockSpec(memory_space=pltpu.SMEM),
            pl.BlockSpec(memory_space=pl.ANY),
            pl.BlockSpec(memory_space=pl.ANY),
        ],
        out_specs=[pl.BlockSpec(memory_space=pltpu.VMEM)] * CHUNKS,
        scratch_shapes=[
            pltpu.VMEM((shots * blocks, LANES, angles), jnp.float32),
            pltpu.VMEM(table.shape, jnp.bfloat16),
            pltpu.SemaphoreType.DMA((shots * blocks + 1,)),
        ],
        compiler_params=pltpu.CompilerParams(vmem_limit_bytes=20 << 20),
        cost_estimate=pl.CostEstimate(
            flops=8 * shots * cycles * angles * LANES, bytes_accessed=frames.size * 4, transcendentals=0
        ),
        name="spectra",
    )(valid_mask, frames, table)


def correlate_kernel(shared, start_ref, *refs):
    n = shared["n"]
    pieces, firsts = refs[:n], refs[n : 2 * n]
    out_ref, centred, pick, weight, inverse = refs[-5:]
    width = out_ref.shape[1]
    cycles = out_ref.shape[2]
    blocks = cycles // LANES
    tail = shared["tail"]
    start = start_ref[0]
    step = pl.program_id(0)

    @pl.when(step == 0)
    def _():
        lane = lax.broadcasted_iota(jnp.int32, (GROUP * width, LANES), 1)
        line = lax.broadcasted_iota(jnp.int32, (GROUP * width, LANES), 0)
        pick[...] = jnp.where(lane == start % LANES + line % width, 1.0, 0.0).astype(jnp.bfloat16)
        total = jnp.zeros((ROWS // 2, LANES), jnp.float32)
        for d in range(n):
            tile = firsts[d][pl.ds(tail, ROWS), :].astype(jnp.float32)
            weight[d] = tile
            total += tile[: ROWS // 2] + tile[ROWS // 2 :]
        inverse[...] = 1.0 / total

    scale = inverse[...]
    for q in range(blocks):
        where = pl.ds(pl.multiple_of((step * blocks + q) * ROWS, ROWS), ROWS)
        total = jnp.zeros((ROWS, LANES), jnp.float32)
        for d in range(n):
            total += pieces[d][where, :].astype(jnp.float32)
        mean = (total[: ROWS // 2] + total[ROWS // 2 :]) * scale
        mean = jnp.concatenate([mean, mean], axis=0)
        for d in range(n):
            tile = (pieces[d][where, :].astype(jnp.float32) - mean) * weight[d]
            centred[pl.ds(d * ROWS, ROWS), pl.ds(q * LANES, LANES)] = tile.astype(jnp.bfloat16)
    own = centred[:, pl.ds(pl.multiple_of(start // LANES * LANES, LANES), LANES)]
    left = lax.dot_general(pick[...], own, (((1,), (1,)), ((), ())), preferred_element_type=jnp.float32)
    line = lax.broadcasted_iota(jnp.int32, left.shape, 0) // width
    lane = lax.broadcasted_iota(jnp.int32, left.shape, 1) % (2 * GROUP) // 2
    left = jnp.where(line == lane, left, 0.0).astype(jnp.bfloat16)
    product = jnp.dot(left, centred[...], preferred_element_type=jnp.float32)
    product = product * scale[:1, :1]
    out_ref[...] = product.reshape(GROUP, width, cycles)


def correlate_call(start, pieces, firsts, before, chunk, cycles, tail):
    n = len(pieces)
    width = cycles // n
    groups = HARMONICS // GROUP // CHUNKS
    operands = [start, *pieces, *firsts]
    specs = [pl.BlockSpec(memory_space=pltpu.SMEM)] + [pl.BlockSpec(memory_space=pltpu.VMEM)] * (2 * n)
    aliases = {}
    if before is not None:
        aliases = {len(operands): 0}
        operands.append(before)
        specs.append(pl.BlockSpec(memory_space=pl.ANY))
    return pl.pallas_call(
        functools.partial(correlate_kernel, {"n": n, "tail": tail}),
        out_shape=jax.ShapeDtypeStruct((HARMONICS, width, cycles), jnp.float32),
        grid=(groups,),
        in_specs=specs,
        out_specs=pl.BlockSpec((GROUP, width, cycles), lambda g: (g + chunk * groups, 0, 0)),
        scratch_shapes=[
            pltpu.VMEM((n * ROWS, cycles), jnp.bfloat16),
            pltpu.VMEM((GROUP * width, LANES), jnp.bfloat16),
            pltpu.VMEM((n, ROWS, LANES), jnp.float32),
            pltpu.VMEM((ROWS // 2, LANES), jnp.float32),
        ],
        input_output_aliases=aliases,
        compiler_params=pltpu.CompilerParams(vmem_limit_bytes=24 << 20),
        cost_estimate=pl.CostEstimate(
            flops=2 * HARMONICS // CHUNKS * width * cycles * n * ROWS,
            bytes_accessed=HARMONICS // CHUNKS * width * cycles * 4,
            transcendentals=0,
        ),
        name="correlate",
    )(*operands)


def gather(piece, n):
    def swap(x, bits):
        return lax.ppermute(x, "pb", [(i, i ^ bits) for i in range(n)])

    held = [piece]
    if n == 16:
        near = swap(piece, 4)
        far = swap(piece, 12)
        held += [near, far, swap(far, 4)]
        held += [swap(x, 2) for x in held]
        held += [swap(x, 1) for x in held]
        return held
    bit = n // 2
    while bit:
        held += [swap(x, bit) for x in held]
        bit //= 2
    return held


def body(frames, valid_mask):
    shots, cycles, angles = frames.shape
    n = lax.axis_size("pb")
    parts = spectra_call(frames, valid_mask)
    start = (lax.axis_index("pb") * (cycles // n)).astype(jnp.int32).reshape(1)
    held = [gather(part, n) for part in parts]
    tail = parts[0].shape[0] - ROWS
    out = None
    for chunk in range(CHUNKS):
        out = correlate_call(start, held[chunk], held[0], out, chunk, cycles, tail)
    return out


def solution(mesh):
    placed = (P(("groups", "pb"), None, None), P(("groups", "pb")))
    return jax.shard_map(
        body, mesh=mesh, in_specs=placed, out_specs=P("groups", "pb", None), check_vma=False
    )
```

time: 198 us -> 65.7 us (0.33)
  waiting for transfers between devices: 107 us -> 20.8 us
  blocking collectives: 35.7 us -> 0 us
  matrix products: 23.2 us -> 0 us
  starting transfers between devices: 0.04 us -> 22.9 us
  Pallas kernels: 0 us -> 16.7 us
  between operations: 13.5 us -> 0.06 us
  other arithmetic: 7.76 us -> 0 us
  local copies, waits for them, and re-layouts: 9.92 us -> 5.08 us
    psum x1 -> x0, waiting for transfers between devices: 55.6 us -> none  [body(): lax.psum((jnp.sum(weights), jnp.sum(spectra.astype(jnp.float32), axis=0))...]
    all_gather x1 -> x0, waiting for transfers between devices: 51.2 us -> none  [body(): piece = lax.all_gather(spectra, 'pb', axis=0, tiled=True)]
    psum x1 -> x0, blocking collectives: 35.7 us -> none  [body(): lax.psum((jnp.sum(weights), jnp.sum(spectra.astype(jnp.float32), axis=0))...]
    dot_general x3 -> x0, matrix products: 23.2 us -> none  [the longest x1 10.2 us: body(): jnp.dot(frames.reshape(shot_dev * cycles, angles), phase_table, precision...]
    ppermute x0 -> x30, starting transfers between devices: none -> 22.9 us  [swap(): return lax.ppermute(x, 'pb', [(i, i ^ bits) for i in range(n)])]
    ppermute x0 -> x30, waiting for transfers between devices: none -> 20.8 us  [swap(): return lax.ppermute(x, 'pb', [(i, i ^ bits) for i in range(n)])]
    pallas_call x0 -> x3, Pallas kernels: none -> 16.7 us  [the longest x2 11.5 us: correlate_call(): pl.pallas_call(functools.partial(correlate_kernel, {'n': n, 'tail': tail}...]
    all_gather x1 -> x0, local copies, waits for them, and re-layouts: 6.43 us -> none  [body(): piece = lax.all_gather(spectra, 'pb', axis=0, tiled=True)]
  transfers between devices with their start and end apart: 2 -> 30, of which waited for: 2 -> 10; matrix products, arithmetic and copies ran while one was open for 1% -> 0% of each run, Pallas kernels for 0% -> 8%
where the time goes in v1:
time: 65.7 us; the launch traced here: 65.5 us
  starting transfers between devices  22.9 us (35%)
  waiting for transfers between devices  20.8 us (32%)
  Pallas kernels  16.7 us (25%)
  local copies, waits for them, and re-layouts  5.08 us (8%)
    ppermute x30, starting transfers between devices, swap(): return lax.ppermute(x, 'pb', [(i, i ^ bits) for i in range(n)])  22.9 us
    ppermute x30, waiting for transfers between devices, swap(): return lax.ppermute(x, 'pb', [(i, i ^ bits) for i in range(n)])  20.8 us
    pallas_call x2, Pallas kernels, correlate_call(): pl.pallas_call(functools.partial(correlate_kernel, {'n': n, 'tail': tail}...  11.5 us
    pallas_call x1, Pallas kernels, spectra_call(): pl.pallas_call(spectra_kernel, out_shape=[jax.ShapeDtypeStruct((r, LANES)...  5.15 us
    unnamed x6, local copies, waits for them, and re-layouts  5.08 us
  transfers between devices with their start and end apart: 30, of which 10 were waited for; matrix products, arithmetic and copies ran while one was open for 0% of the time, Pallas kernels for 8%

profile of v1, /device:TPU:0, one launch (start us, length us, event | category | flops | bytes accessed | tf_op | source)
XLA Modules:
  0.0 65.5 jit_solution(10735020770642492260)
XLA Ops:
  0.0 3.4 %copy-done = f32[2,512,2048]{2,1,0:T(8,128)S(1)} copy-done((f32[2,512,2048]{2,1,0:T(8,128)S(1)}, f32[2,512,2048]{2,1,0:T(8,128)}, u32[]{:S(2)}) %copy-start) | copy-done | bytes 8388632
  3.4 1.0 %copy-done.1 = bf16[1024,256]{1,0:T(8,128)(2,1)S(1)} copy-done((bf16[1024,256]{1,0:T(8,128)(2,1)S(1)}, bf16[1024,256]{1,0:T(8,128)(2,1)}, u32[]{:S(2)}) %copy-start.1) | copy-done | bytes 524312
  4.4 0.7 copy-done.2
  5.1 5.1 %spectra.1 = (bf16[528,128]{1,0:T(8,128)(2,1)S(1)}, bf16[512,128]{1,0:T(8,128)(2,1)S(1)}) custom-call(s32[2]{0:T(128)S(1)} %copy-done.2, f32[2,512,2048]{2,1,0:T(8,128)S(1)} %copy-done, bf16[1024,256]{1,0:T(8,128)(2,1)S(1)} %copy-done.1), custom_call_target="tpu_custom_call" | custom-call | flops 2147483648 | bytes 8388608 | tf_op jit(solution)/shard_map/spectra/pallas_call | solution.py:76
  10.2 0.6 collective-permute-start.7
  10.8 2.6 %collective-permute-start.3 = (bf16[512,128]{1,0:T(8,128)(2,1)S(1)}, bf16[512,128]{1,0:T(8,128)(2,1)S(1)}, u32[]{:S(2)}, u32[]{:S(2)}) collective-permute-start(bf16[512,128]{1,0:T(8,128)(2,1)S(1)} %get-tuple-element.7.refs_0_), channel_id=1, source_target_pairs={{0,2},{1,3},{2,0},{3,1},{4,6},{5,7},{6,4},{7,5},{8,10},{9,11},{10,... | collective-permute-start | bytes 393224 | tf_op jit(solution)/shard_map/ppermute | solution.py:178
  13.4 3.6 %collective-permute-start.1 = (bf16[512,128]{1,0:T(8,128)(2,1)S(1)}, bf16[512,128]{1,0:T(8,128)(2,1)S(1)}, u32[]{:S(2)}, u32[]{:S(2)}) collective-permute-start(bf16[512,128]{1,0:T(8,128)(2,1)S(1)} %get-tuple-element.7.refs_0_), channel_id=1, source_target_pairs={{0,12},{1,13},{2,14},{3,15},{4,8},{5,9},{6,10},{7,11},{8,4},{9,5},... | collective-permute-start | bytes 393224 | tf_op jit(solution)/shard_map/ppermute | solution.py:178
  17.0 0.0 collective-permute-start.22
  17.0 0.0 collective-permute-start
  17.0 0.0 collective-permute-done.7.refs_8_
  17.0 0.9 %collective-permute-start.16 = (bf16[528,128]{1,0:T(8,128)(2,1)S(1)}, bf16[528,128]{1,0:T(8,128)(2,1)S(1)}, u32[]{:S(2)}, u32[]{:S(2)}) collective-permute-start(bf16[528,128]{1,0:T(8,128)(2,1)S(1)} %get-tuple-element.8.refs_0_.refs_16_), channel_id=1, source_target_pairs={{0,12},{1,13},{2,14},{3,15},{4,8},{5,9},{6,10},{7,11},{8,4},{9,5},... | collective-permute-start | bytes 405512 | tf_op jit(solution)/shard_map/ppermute | solution.py:178
  17.9 1.3 %collective-permute-start.18 = (bf16[528,128]{1,0:T(8,128)(2,1)S(1)}, bf16[528,128]{1,0:T(8,128)(2,1)S(1)}, u32[]{:S(2)}, u32[]{:S(2)}) collective-permute-start(bf16[528,128]{1,0:T(8,128)(2,1)S(1)} %get-tuple-element.8.refs_0_.refs_16_), channel_id=1, source_target_pairs={{0,2},{1,3},{2,0},{3,1},{4,6},{5,7},{6,4},{7,5},{8,10},{9,11},{10,... | collective-permute-start | bytes 405512 | tf_op jit(solution)/shard_map/ppermute | solution.py:178
  19.2 2.4 %collective-permute-done.1.refs_2_ = bf16[512,128]{1,0:T(8,128)(2,1)S(1)} collective-permute-done((bf16[512,128]{1,0:T(8,128)(2,1)S(1)}, bf16[512,128]{1,0:T(8,128)(2,1)S(1)}, u32[]{:S(2)}, u32[]{:S(2)}) %collective-permute-start.1) | collective-permute-done | bytes 131104 | tf_op jit(solution)/shard_map/ppermute | solution.py:178
  21.6 3.2 %collective-permute-start.15 = (bf16[528,128]{1,0:T(8,128)(2,1)S(1)}, bf16[528,128]{1,0:T(8,128)(2,1)S(1)}, u32[]{:S(2)}, u32[]{:S(2)}) collective-permute-start(bf16[528,128]{1,0:T(8,128)(2,1)S(1)} %get-tuple-element.8.refs_0_.refs_16_), channel_id=1, source_target_pairs={{0,4},{1,5},{2,6},{3,7},{4,0},{5,1},{6,2},{7,3},{8,12},{9,13},{10,... | collective-permute-start | bytes 405512 | tf_op jit(solution)/shard_map/ppermute | solution.py:178
  24.8 1.4 %collective-permute-done.refs_1_ = bf16[512,128]{1,0:T(8,128)(2,1)S(1)} collective-permute-done((bf16[512,128]{1,0:T(8,128)(2,1)S(1)}, bf16[512,128]{1,0:T(8,128)(2,1)S(1)}, u32[]{:S(2)}, u32[]{:S(2)}) %collective-permute-start) | collective-permute-done | bytes 131104 | tf_op jit(solution)/shard_map/ppermute | solution.py:178
  26.2 0.5 collective-permute-start.9
  26.7 0.6 collective-permute-done.16.refs_2_.refs_18_
  27.3 1.8 %collective-permute-start.17 = (bf16[528,128]{1,0:T(8,128)(2,1)S(1)}, bf16[528,128]{1,0:T(8,128)(2,1)S(1)}, u32[]{:S(2)}, u32[]{:S(2)}) collective-permute-start(bf16[528,128]{1,0:T(8,128)(2,1)S(1)} %collective-permute-done.16.refs_2_.refs_18_), channel_id=1, source_target_pairs={{0,4},{1,5},{2,6},{3,7},{4,0},{5,1},{6,2},{7,3},{8,12},{9,13},{10,... | collective-permute-start | bytes 405512 | tf_op jit(solution)/shard_map/ppermute | solution.py:178
  29.1 0.0 collective-permute-done.18.refs_4_.refs_20_
  29.1 0.0 collective-permute-start.26
  29.1 0.5 collective-permute-done.15.refs_1_.refs_17_
  29.6 0.5 collective-permute-start.5
  30.1 1.9 %collective-permute-start.2 = (bf16[512,128]{1,0:T(8,128)(2,1)S(1)}, bf16[512,128]{1,0:T(8,128)(2,1)S(1)}, u32[]{:S(2)}, u32[]{:S(2)}) collective-permute-start(bf16[512,128]{1,0:T(8,128)(2,1)S(1)} %collective-permute-done.1.refs_2_), channel_id=1, source_target_pairs={{0,4},{1,5},{2,6},{3,7},{4,0},{5,1},{6,2},{7,3},{8,12},{9,13},{10,... | collective-permute-start | bytes 393224 | tf_op jit(solution)/shard_map/ppermute | solution.py:178
  32.0 1.5 %collective-permute-start.4 = (bf16[512,128]{1,0:T(8,128)(2,1)S(1)}, bf16[512,128]{1,0:T(8,128)(2,1)S(1)}, u32[]{:S(2)}, u32[]{:S(2)}) collective-permute-start(bf16[512,128]{1,0:T(8,128)(2,1)S(1)} %collective-permute-done.refs_1_), channel_id=1, source_target_pairs={{0,2},{1,3},{2,0},{3,1},{4,6},{5,7},{6,4},{7,5},{8,10},{9,11},{10,... | collective-permute-start | bytes 393224 | tf_op jit(solution)/shard_map/ppermute | solution.py:178
  33.5 2.5 %collective-permute-done.5.refs_6_ = bf16[512,128]{1,0:T(8,128)(2,1)S(1)} collective-permute-done((bf16[512,128]{1,0:T(8,128)(2,1)S(1)}, bf16[512,128]{1,0:T(8,128)(2,1)S(1)}, u32[]{:S(2)}, u32[]{:S(2)}) %collective-permute-start.5) | collective-permute-done | bytes 131104 | tf_op jit(solution)/shard_map/ppermute | solution.py:178
  36.0 0.5 collective-permute-start.20
  36.4 0.0 collective-permute-done.2.refs_3_
  36.4 0.0 collective-permute-start.24
  36.4 2.3 %collective-permute-done.4.refs_5_ = bf16[512,128]{1,0:T(8,128)(2,1)S(1)} collective-permute-done((bf16[512,128]{1,0:T(8,128)(2,1)S(1)}, bf16[512,128]{1,0:T(8,128)(2,1)S(1)}, u32[]{:S(2)}, u32[]{:S(2)}) %collective-permute-start.4) | collective-permute-done | bytes 131104 | tf_op jit(solution)/shard_map/ppermute | solution.py:178
  38.8 0.8 %collective-permute-start.19 = (bf16[528,128]{1,0:T(8,128)(2,1)S(1)}, bf16[528,128]{1,0:T(8,128)(2,1)S(1)}, u32[]{:S(2)}, u32[]{:S(2)}) collective-permute-start(bf16[528,128]{1,0:T(8,128)(2,1)S(1)} %collective-permute-done.15.refs_1_.refs_17_), channel_id=1, source_target_pairs={{0,2},{1,3},{2,0},{3,1},{4,6},{5,7},{6,4},{7,5},{8,10},{9,11},{10,... | collective-permute-start | bytes 405512 | tf_op jit(solution)/shard_map/ppermute | solution.py:178
  39.6 1.3 %collective-permute-start.21 = (bf16[528,128]{1,0:T(8,128)(2,1)S(1)}, bf16[528,128]{1,0:T(8,128)(2,1)S(1)}, u32[]{:S(2)}, u32[]{:S(2)}) collective-permute-start(bf16[528,128]{1,0:T(8,128)(2,1)S(1)} %collective-permute-done.17.refs_3_.refs_19_), channel_id=1, source_target_pairs={{0,2},{1,3},{2,0},{3,1},{4,6},{5,7},{6,4},{7,5},{8,10},{9,11},{10,... | collective-permute-start | bytes 405512 | tf_op jit(solution)/shard_map/ppermute | solution.py:178
  40.8 0.0 collective-permute-done.26.refs_12_.refs_28_
  40.8 0.0 collective-permute-start.23
  40.8 1.6 %collective-permute-done.20.refs_6_.refs_22_ = bf16[528,128]{1,0:T(8,128)(2,1)S(1)} collective-permute-done((bf16[528,128]{1,0:T(8,128)(2,1)S(1)}, bf16[528,128]{1,0:T(8,128)(2,1)S(1)}, u32[]{:S(2)}, u32[]{:S(2)}) %collective-permute-start.20) | collective-permute-done | bytes 135200 | tf_op jit(solution)/shard_map/ppermute | solution.py:178
  42.4 0.0 collective-permute-done.24.refs_10_.refs_26_
  42.4 0.5 collective-permute-start.25
  42.9 2.4 %collective-permute-done.19.refs_5_.refs_21_ = bf16[528,128]{1,0:T(8,128)(2,1)S(1)} collective-permute-done((bf16[528,128]{1,0:T(8,128)(2,1)S(1)}, bf16[528,128]{1,0:T(8,128)(2,1)S(1)}, u32[]{:S(2)}, u32[]{:S(2)}) %collective-permute-start.19) | collective-permute-done | bytes 135200 | tf_op jit(solution)/shard_map/ppermute | solution.py:178
  45.3 0.0 collective-permute-start.27
  45.3 1.5 %collective-permute-done.21.refs_7_.refs_23_ = bf16[528,128]{1,0:T(8,128)(2,1)S(1)} collective-permute-done((bf16[528,128]{1,0:T(8,128)(2,1)S(1)}, bf16[528,128]{1,0:T(8,128)(2,1)S(1)}, u32[]{:S(2)}, u32[]{:S(2)}) %collective-permute-start.21) | collective-permute-done | bytes 135200 | tf_op jit(solution)/shard_map/ppermute | solution.py:178
  46.8 0.0 collective-permute-start.29
  46.8 0.5 collective-permute-start.6
  47.2 5.6 %collective-permute-done.6.refs_7_ = bf16[512,128]{1,0:T(8,128)(2,1)} collective-permute-done((bf16[512,128]{1,0:T(8,128)(2,1)S(1)}, bf16[512,128]{1,0:T(8,128)(2,1)}, u32[]{:S(2)}, u32[]{:S(2)}) %collective-permute-start.6) | collective-permute-done | bytes 131104 | tf_op jit(solution)/shard_map/ppermute | solution.py:178
  52.8 0.5 collective-permute-start.10
  53.3 0.1 collective-permute-start.13
  53.4 0.4 collective-permute-start.12
  53.8 0.1 collective-permute-start.14
  53.9 5.1 %correlate.2.refs_32_ = f32[64,32,512]{2,1,0:T(8,128)} custom-call(s32[1]{0:T(128)} %bitcast.start_ref, bf16[528,128]{1,0:T(8,128)(2,1)S(1)} %get-tuple-element.8.refs_0_.refs_16_, bf16[528,128]{1,0:T(8,128)(2,1)S(1)} %collective-permute-done.15.refs_1_.refs_17_, bf16[528,128]{1,0:T(8,128)(2,1)S(1)} %collective-permute-done.16.refs_2_.refs_18_, ...), custom_call_target="tpu_custom_call" | custom-call | flops 268435456 | bytes 2097152 | tf_op jit(solution)/shard_map/correlate/pallas_call | solution.py:153
  59.1 6.4 %correlate.3 = f32[64,32,512]{2,1,0:T(8,128)} custom-call(s32[1]{0:T(128)} %bitcast.start_ref, bf16[512,128]{1,0:T(8,128)(2,1)S(1)} %get-tuple-element.7.refs_0_, bf16[512,128]{1,0:T(8,128)(2,1)S(1)} %collective-permute-done.refs_1_, bf16[512,128]{1,0:T(8,128)(2,1)S(1)} %collective-permute-done.1.refs_2_, ...), custom_call_target="tpu_custom_call", output_to_operand_aliasing={{}: (33, {})} | custom-call | flops 268435456 | bytes 2097152 | tf_op jit(solution)/shard_map/correlate/pallas_call | solution.py:153
  (21 shorter events, 0.1 us)
Async XLA Ops:
  0.0 3.4 %copy-start = (f32[2,512,2048]{2,1,0:T(8,128)S(1)}, f32[2,512,2048]{2,1,0:T(8,128)}, u32[]{:S(2)}) copy-start(f32[2,512,2048]{2,1,0:T(8,128)} %frames_ref.1) | copy-start | bytes 25165828
  3.4 1.0 %copy-start.1 = (bf16[1024,256]{1,0:T(8,128)(2,1)S(1)}, bf16[1024,256]{1,0:T(8,128)(2,1)}, u32[]{:S(2)}) copy-start(bf16[1024,256]{1,0:T(8,128)(2,1)} %constant.8.clone.table_ref) | copy-start | bytes 1572868
  4.4 0.7 %copy-start.2 = (s32[2]{0:T(128)S(1)}, s32[2]{0:T(128)}, u32[]{:S(2)}) copy-start(s32[2]{0:T(128)} %mask_ref.1) | copy-start | bytes 28
  10.2 6.8 %collective-permute-start.7 = (bf16[512,128]{1,0:T(8,128)(2,1)S(1)}, bf16[512,128]{1,0:T(8,128)(2,1)S(1)}, u32[]{:S(2)}, u32[]{:S(2)}) collective-permute-start(bf16[512,128]{1,0:T(8,128)(2,1)S(1)} %get-tuple-element.7.refs_0_), channel_id=1, source_target_pairs={{0,1},{1,0},{2,3},{3,2},{4,5},{5,4},{6,7},{7,6},{8,9},{9,8},{10,11... | collective-permute-start | bytes 393224 | tf_op jit(solution)/shard_map/ppermute | solution.py:178
  10.8 7.1 %collective-permute-start.3 = (bf16[512,128]{1,0:T(8,128)(2,1)S(1)}, bf16[512,128]{1,0:T(8,128)(2,1)S(1)}, u32[]{:S(2)}, u32[]{:S(2)}) collective-permute-start(bf16[512,128]{1,0:T(8,128)(2,1)S(1)} %get-tuple-element.7.refs_0_), channel_id=1, source_target_pairs={{0,2},{1,3},{2,0},{3,1},{4,6},{5,7},{6,4},{7,5},{8,10},{9,11},{10,... | collective-permute-start | bytes 393224 | tf_op jit(solution)/shard_map/ppermute | solution.py:178
  13.4 8.2 %collective-permute-start.1 = (bf16[512,128]{1,0:T(8,128)(2,1)S(1)}, bf16[512,128]{1,0:T(8,128)(2,1)S(1)}, u32[]{:S(2)}, u32[]{:S(2)}) collective-permute-start(bf16[512,128]{1,0:T(8,128)(2,1)S(1)} %get-tuple-element.7.refs_0_), channel_id=1, source_target_pairs={{0,12},{1,13},{2,14},{3,15},{4,8},{5,9},{6,10},{7,11},{8,4},{9,5},... | collective-permute-start | bytes 393224 | tf_op jit(solution)/shard_map/ppermute | solution.py:178
  17.0 9.2 %collective-permute-start.22 = (bf16[528,128]{1,0:T(8,128)(2,1)S(1)}, bf16[528,128]{1,0:T(8,128)(2,1)S(1)}, u32[]{:S(2)}, u32[]{:S(2)}) collective-permute-start(bf16[528,128]{1,0:T(8,128)(2,1)S(1)} %get-tuple-element.8.refs_0_.refs_16_), channel_id=1, source_target_pairs={{0,1},{1,0},{2,3},{3,2},{4,5},{5,4},{6,7},{7,6},{8,9},{9,8},{10,11... | collective-permute-start | bytes 405512 | tf_op jit(solution)/shard_map/ppermute | solution.py:178
  17.0 9.2 %collective-permute-start = (bf16[512,128]{1,0:T(8,128)(2,1)S(1)}, bf16[512,128]{1,0:T(8,128)(2,1)S(1)}, u32[]{:S(2)}, u32[]{:S(2)}) collective-permute-start(bf16[512,128]{1,0:T(8,128)(2,1)S(1)} %get-tuple-element.7.refs_0_), channel_id=1, source_target_pairs={{0,4},{1,5},{2,6},{3,7},{4,0},{5,1},{6,2},{7,3},{8,12},{9,13},{10,... | collective-permute-start | bytes 393224 | tf_op jit(solution)/shard_map/ppermute | solution.py:178
  17.0 10.4 %collective-permute-start.16 = (bf16[528,128]{1,0:T(8,128)(2,1)S(1)}, bf16[528,128]{1,0:T(8,128)(2,1)S(1)}, u32[]{:S(2)}, u32[]{:S(2)}) collective-permute-start(bf16[528,128]{1,0:T(8,128)(2,1)S(1)} %get-tuple-element.8.refs_0_.refs_16_), channel_id=1, source_target_pairs={{0,12},{1,13},{2,14},{3,15},{4,8},{5,9},{6,10},{7,11},{8,4},{9,5},... | collective-permute-start | bytes 405512 | tf_op jit(solution)/shard_map/ppermute | solution.py:178
  17.9 11.2 %collective-permute-start.18 = (bf16[528,128]{1,0:T(8,128)(2,1)S(1)}, bf16[528,128]{1,0:T(8,128)(2,1)S(1)}, u32[]{:S(2)}, u32[]{:S(2)}) collective-permute-start(bf16[528,128]{1,0:T(8,128)(2,1)S(1)} %get-tuple-element.8.refs_0_.refs_16_), channel_id=1, source_target_pairs={{0,2},{1,3},{2,0},{3,1},{4,6},{5,7},{6,4},{7,5},{8,10},{9,11},{10,... | collective-permute-start | bytes 405512 | tf_op jit(solution)/shard_map/ppermute | solution.py:178
  21.6 8.0 %collective-permute-start.15 = (bf16[528,128]{1,0:T(8,128)(2,1)S(1)}, bf16[528,128]{1,0:T(8,128)(2,1)S(1)}, u32[]{:S(2)}, u32[]{:S(2)}) collective-permute-start(bf16[528,128]{1,0:T(8,128)(2,1)S(1)} %get-tuple-element.8.refs_0_.refs_16_), channel_id=1, source_target_pairs={{0,4},{1,5},{2,6},{3,7},{4,0},{5,1},{6,2},{7,3},{8,12},{9,13},{10,... | collective-permute-start | bytes 405512 | tf_op jit(solution)/shard_map/ppermute | solution.py:178
  26.2 3.9 %collective-permute-start.11 = (bf16[512,128]{1,0:T(8,128)(2,1)S(1)}, bf16[512,128]{1,0:T(8,128)(2,1)S(1)}, u32[]{:S(2)}, u32[]{:S(2)}) collective-permute-start(bf16[512,128]{1,0:T(8,128)(2,1)S(1)} %collective-permute-done.3.refs_4_), channel_id=1, source_target_pairs={{0,1},{1,0},{2,3},{3,2},{4,5},{5,4},{6,7},{7,6},{8,9},{9,8},{10,11... | collective-permute-start | bytes 393224 | tf_op jit(solution)/shard_map/ppermute | solution.py:178
  26.2 5.8 %collective-permute-start.9 = (bf16[512,128]{1,0:T(8,128)(2,1)S(1)}, bf16[512,128]{1,0:T(8,128)(2,1)S(1)}, u32[]{:S(2)}, u32[]{:S(2)}) collective-permute-start(bf16[512,128]{1,0:T(8,128)(2,1)S(1)} %collective-permute-done.1.refs_2_), channel_id=1, source_target_pairs={{0,1},{1,0},{2,3},{3,2},{4,5},{5,4},{6,7},{7,6},{8,9},{9,8},{10,11... | collective-permute-start | bytes 393224 | tf_op jit(solution)/shard_map/ppermute | solution.py:178
  27.3 12.2 %collective-permute-start.17 = (bf16[528,128]{1,0:T(8,128)(2,1)S(1)}, bf16[528,128]{1,0:T(8,128)(2,1)S(1)}, u32[]{:S(2)}, u32[]{:S(2)}) collective-permute-start(bf16[528,128]{1,0:T(8,128)(2,1)S(1)} %collective-permute-done.16.refs_2_.refs_18_), channel_id=1, source_target_pairs={{0,4},{1,5},{2,6},{3,7},{4,0},{5,1},{6,2},{7,3},{8,12},{9,13},{10,... | collective-permute-start | bytes 405512 | tf_op jit(solution)/shard_map/ppermute | solution.py:178
  29.1 11.7 %collective-permute-start.26 = (bf16[528,128]{1,0:T(8,128)(2,1)S(1)}, bf16[528,128]{1,0:T(8,128)(2,1)S(1)}, u32[]{:S(2)}, u32[]{:S(2)}) collective-permute-start(bf16[528,128]{1,0:T(8,128)(2,1)S(1)} %collective-permute-done.18.refs_4_.refs_20_), channel_id=1, source_target_pairs={{0,1},{1,0},{2,3},{3,2},{4,5},{5,4},{6,7},{7,6},{8,9},{9,8},{10,11... | collective-permute-start | bytes 405512 | tf_op jit(solution)/shard_map/ppermute | solution.py:178
  29.6 6.4 %collective-permute-start.5 = (bf16[512,128]{1,0:T(8,128)(2,1)S(1)}, bf16[512,128]{1,0:T(8,128)(2,1)S(1)}, u32[]{:S(2)}, u32[]{:S(2)}) collective-permute-start(bf16[512,128]{1,0:T(8,128)(2,1)S(1)} %collective-permute-done.1.refs_2_), channel_id=1, source_target_pairs={{0,2},{1,3},{2,0},{3,1},{4,6},{5,7},{6,4},{7,5},{8,10},{9,11},{10,... | collective-permute-start | bytes 393224 | tf_op jit(solution)/shard_map/ppermute | solution.py:178
  30.1 6.4 %collective-permute-start.2 = (bf16[512,128]{1,0:T(8,128)(2,1)S(1)}, bf16[512,128]{1,0:T(8,128)(2,1)S(1)}, u32[]{:S(2)}, u32[]{:S(2)}) collective-permute-start(bf16[512,128]{1,0:T(8,128)(2,1)S(1)} %collective-permute-done.1.refs_2_), channel_id=1, source_target_pairs={{0,4},{1,5},{2,6},{3,7},{4,0},{5,1},{6,2},{7,3},{8,12},{9,13},{10,... | collective-permute-start | bytes 393224 | tf_op jit(solution)/shard_map/ppermute | solution.py:178
  32.0 6.8 %collective-permute-start.4 = (bf16[512,128]{1,0:T(8,128)(2,1)S(1)}, bf16[512,128]{1,0:T(8,128)(2,1)S(1)}, u32[]{:S(2)}, u32[]{:S(2)}) collective-permute-start(bf16[512,128]{1,0:T(8,128)(2,1)S(1)} %collective-permute-done.refs_1_), channel_id=1, source_target_pairs={{0,2},{1,3},{2,0},{3,1},{4,6},{5,7},{6,4},{7,5},{8,10},{9,11},{10,... | collective-permute-start | bytes 393224 | tf_op jit(solution)/shard_map/ppermute | solution.py:178
  36.0 6.4 %collective-permute-start.20 = (bf16[528,128]{1,0:T(8,128)(2,1)S(1)}, bf16[528,128]{1,0:T(8,128)(2,1)S(1)}, u32[]{:S(2)}, u32[]{:S(2)}) collective-permute-start(bf16[528,128]{1,0:T(8,128)(2,1)S(1)} %collective-permute-done.16.refs_2_.refs_18_), channel_id=1, source_target_pairs={{0,2},{1,3},{2,0},{3,1},{4,6},{5,7},{6,4},{7,5},{8,10},{9,11},{10,... | collective-permute-start | bytes 405512 | tf_op jit(solution)/shard_map/ppermute | solution.py:178
  36.4 6.0 %collective-permute-start.24 = (bf16[528,128]{1,0:T(8,128)(2,1)S(1)}, bf16[528,128]{1,0:T(8,128)(2,1)S(1)}, u32[]{:S(2)}, u32[]{:S(2)}) collective-permute-start(bf16[528,128]{1,0:T(8,128)(2,1)S(1)} %collective-permute-done.16.refs_2_.refs_18_), channel_id=1, source_target_pairs={{0,1},{1,0},{2,3},{3,2},{4,5},{5,4},{6,7},{7,6},{8,9},{9,8},{10,11... | collective-permute-start | bytes 405512 | tf_op jit(solution)/shard_map/ppermute | solution.py:178
  38.8 6.5 %collective-permute-start.19 = (bf16[528,128]{1,0:T(8,128)(2,1)S(1)}, bf16[528,128]{1,0:T(8,128)(2,1)S(1)}, u32[]{:S(2)}, u32[]{:S(2)}) collective-permute-start(bf16[528,128]{1,0:T(8,128)(2,1)S(1)} %collective-permute-done.15.refs_1_.refs_17_), channel_id=1, source_target_pairs={{0,2},{1,3},{2,0},{3,1},{4,6},{5,7},{6,4},{7,5},{8,10},{9,11},{10,... | collective-permute-start | bytes 405512 | tf_op jit(solution)/shard_map/ppermute | solution.py:178
  39.6 7.2 %collective-permute-start.21 = (bf16[528,128]{1,0:T(8,128)(2,1)S(1)}, bf16[528,128]{1,0:T(8,128)(2,1)S(1)}, u32[]{:S(2)}, u32[]{:S(2)}) collective-permute-start(bf16[528,128]{1,0:T(8,128)(2,1)S(1)} %collective-permute-done.17.refs_3_.refs_19_), channel_id=1, source_target_pairs={{0,2},{1,3},{2,0},{3,1},{4,6},{5,7},{6,4},{7,5},{8,10},{9,11},{10,... | collective-permute-start | bytes 405512 | tf_op jit(solution)/shard_map/ppermute | solution.py:178
  40.8 6.0 %collective-permute-start.23 = (bf16[528,128]{1,0:T(8,128)(2,1)S(1)}, bf16[528,128]{1,0:T(8,128)(2,1)S(1)}, u32[]{:S(2)}, u32[]{:S(2)}) collective-permute-start(bf16[528,128]{1,0:T(8,128)(2,1)S(1)} %collective-permute-done.15.refs_1_.refs_17_), channel_id=1, source_target_pairs={{0,1},{1,0},{2,3},{3,2},{4,5},{5,4},{6,7},{7,6},{8,9},{9,8},{10,11... | collective-permute-start | bytes 405512 | tf_op jit(solution)/shard_map/ppermute | solution.py:178
  42.4 10.4 %collective-permute-start.28 = (bf16[528,128]{1,0:T(8,128)(2,1)S(1)}, bf16[528,128]{1,0:T(8,128)(2,1)S(1)}, u32[]{:S(2)}, u32[]{:S(2)}) collective-permute-start(bf16[528,128]{1,0:T(8,128)(2,1)S(1)} %collective-permute-done.20.refs_6_.refs_22_), channel_id=1, source_target_pairs={{0,1},{1,0},{2,3},{3,2},{4,5},{5,4},{6,7},{7,6},{8,9},{9,8},{10,11... | collective-permute-start | bytes 405512 | tf_op jit(solution)/shard_map/ppermute | solution.py:178
  42.4 10.9 %collective-permute-start.25 = (bf16[528,128]{1,0:T(8,128)(2,1)S(1)}, bf16[528,128]{1,0:T(8,128)(2,1)S(1)}, u32[]{:S(2)}, u32[]{:S(2)}) collective-permute-start(bf16[528,128]{1,0:T(8,128)(2,1)S(1)} %collective-permute-done.17.refs_3_.refs_19_), channel_id=1, source_target_pairs={{0,1},{1,0},{2,3},{3,2},{4,5},{5,4},{6,7},{7,6},{8,9},{9,8},{10,11... | collective-permute-start | bytes 405512 | tf_op jit(solution)/shard_map/ppermute | solution.py:178
  45.3 8.1 %collective-permute-start.27 = (bf16[528,128]{1,0:T(8,128)(2,1)S(1)}, bf16[528,128]{1,0:T(8,128)(2,1)S(1)}, u32[]{:S(2)}, u32[]{:S(2)}) collective-permute-start(bf16[528,128]{1,0:T(8,128)(2,1)S(1)} %collective-permute-done.19.refs_5_.refs_21_), channel_id=1, source_target_pairs={{0,1},{1,0},{2,3},{3,2},{4,5},{5,4},{6,7},{7,6},{8,9},{9,8},{10,11... | collective-permute-start | bytes 405512 | tf_op jit(solution)/shard_map/ppermute | solution.py:178
  46.8 7.1 %collective-permute-start.29 = (bf16[528,128]{1,0:T(8,128)(2,1)S(1)}, bf16[528,128]{1,0:T(8,128)(2,1)S(1)}, u32[]{:S(2)}, u32[]{:S(2)}) collective-permute-start(bf16[528,128]{1,0:T(8,128)(2,1)S(1)} %collective-permute-done.21.refs_7_.refs_23_), channel_id=1, source_target_pairs={{0,1},{1,0},{2,3},{3,2},{4,5},{5,4},{6,7},{7,6},{8,9},{9,8},{10,11... | collective-permute-start | bytes 405512 | tf_op jit(solution)/shard_map/ppermute | solution.py:178
  46.8 6.0 %collective-permute-start.6 = (bf16[512,128]{1,0:T(8,128)(2,1)S(1)}, bf16[512,128]{1,0:T(8,128)(2,1)}, u32[]{:S(2)}, u32[]{:S(2)}) collective-permute-start(bf16[512,128]{1,0:T(8,128)(2,1)S(1)} %collective-permute-done.2.refs_3_), channel_id=1, source_target_pairs={{0,2},{1,3},{2,0},{3,1},{4,6},{5,7},{6,4},{7,5},{8,10},{9,11},{10,... | collective-permute-start | bytes 393224 | tf_op jit(solution)/shard_map/ppermute | solution.py:178
  52.8 6.2 %collective-permute-start.8 = (bf16[512,128]{1,0:T(8,128)(2,1)S(1)}, bf16[512,128]{1,0:T(8,128)(2,1)}, u32[]{:S(2)}, u32[]{:S(2)}) collective-permute-start(bf16[512,128]{1,0:T(8,128)(2,1)S(1)} %collective-permute-done.refs_1_), channel_id=1, source_target_pairs={{0,1},{1,0},{2,3},{3,2},{4,5},{5,4},{6,7},{7,6},{8,9},{9,8},{10,11... | collective-permute-start | bytes 393224 | tf_op jit(solution)/shard_map/ppermute | solution.py:178
  52.8 6.2 %collective-permute-start.10 = (bf16[512,128]{1,0:T(8,128)(2,1)S(1)}, bf16[512,128]{1,0:T(8,128)(2,1)}, u32[]{:S(2)}, u32[]{:S(2)}) collective-permute-start(bf16[512,128]{1,0:T(8,128)(2,1)S(1)} %collective-permute-done.2.refs_3_), channel_id=1, source_target_pairs={{0,1},{1,0},{2,3},{3,2},{4,5},{5,4},{6,7},{7,6},{8,9},{9,8},{10,11... | collective-permute-start | bytes 393224 | tf_op jit(solution)/shard_map/ppermute | solution.py:178
  53.3 5.7 %collective-permute-start.13 = (bf16[512,128]{1,0:T(8,128)(2,1)S(1)}, bf16[512,128]{1,0:T(8,128)(2,1)}, u32[]{:S(2)}, u32[]{:S(2)}) collective-permute-start(bf16[512,128]{1,0:T(8,128)(2,1)S(1)} %collective-permute-done.5.refs_6_), channel_id=1, source_target_pairs={{0,1},{1,0},{2,3},{3,2},{4,5},{5,4},{6,7},{7,6},{8,9},{9,8},{10,11... | collective-permute-start | bytes 393224 | tf_op jit(solution)/shard_map/ppermute | solution.py:178
  53.4 5.6 %collective-permute-start.12 = (bf16[512,128]{1,0:T(8,128)(2,1)S(1)}, bf16[512,128]{1,0:T(8,128)(2,1)}, u32[]{:S(2)}, u32[]{:S(2)}) collective-permute-start(bf16[512,128]{1,0:T(8,128)(2,1)S(1)} %collective-permute-done.4.refs_5_), channel_id=1, source_target_pairs={{0,1},{1,0},{2,3},{3,2},{4,5},{5,4},{6,7},{7,6},{8,9},{9,8},{10,11... | collective-permute-start | bytes 393224 | tf_op jit(solution)/shard_map/ppermute | solution.py:178
  53.8 5.2 %collective-permute-start.14 = (bf16[512,128]{1,0:T(8,128)(2,1)}, bf16[512,128]{1,0:T(8,128)(2,1)}, u32[]{:S(2)}, u32[]{:S(2)}) collective-permute-start(bf16[512,128]{1,0:T(8,128)(2,1)} %collective-permute-done.6.refs_7_), channel_id=1, source_target_pairs={{0,1},{1,0},{2,3},{3,2},{4,5},{5,4},{6,7},{7,6},{8,9},{9,8},{10,11... | collective-permute-start | bytes 393224 | tf_op jit(solution)/shard_map/ppermute | solution.py:178

commit v2 on v1

v2 whole, which is shorter than its diff:
```python
import functools
import math

import jax
import jax.numpy as jnp
import numpy as np
from jax import lax
from jax.experimental import pallas as pl
from jax.experimental.pallas import tpu as pltpu
from jax.sharding import PartitionSpec as P

HARMONICS = 64
LANES = 128
GROUP = 4
ROWS = 4 * GROUP
CHUNKS = 2
DEPTH = 256


def half_table(angles):
    order = 2 * (np.arange(HARMONICS) + 1)
    wrapped = np.arange(angles // 2)[:, None] * order[None, :] % angles
    phase = wrapped * (2.0 * math.pi / angles)
    table = np.stack([np.cos(phase), -np.sin(phase)], axis=-1).reshape(angles // 2, 2 * HARMONICS)
    table = (2.0 / math.sqrt(angles)) * table
    high = table.astype(jnp.bfloat16)
    low = (table - high.astype(np.float64)).astype(jnp.bfloat16)
    return np.concatenate([high, low], axis=1)


def spectra_kernel(mask_ref, frames_ref, table_ref, *refs):
    out_refs = refs[:CHUNKS]
    buf, table, halves, sems = refs[CHUNKS:]
    shots, cycles, angles = frames_ref.shape
    blocks = cycles // LANES
    half = angles // 2
    groups = HARMONICS // GROUP // CHUNKS
    copies = [pltpu.make_async_copy(table_ref, table, sems.at[shots * blocks])]
    for q in range(blocks):
        for s in range(shots):
            copies.append(
                pltpu.make_async_copy(
                    frames_ref.at[s, pl.ds(q * LANES, LANES), :], buf.at[q * shots + s], sems.at[q * shots + s]
                )
            )
    for copy in copies:
        copy.start()
    weights = [mask_ref[s].astype(jnp.float32) for s in range(shots)]
    row = lax.broadcasted_iota(jnp.int32, (ROWS, LANES), 0)
    tile = jnp.where(row < ROWS // 2, weights[0], weights[1]).astype(jnp.bfloat16)
    out_refs[0][pl.ds(groups * blocks * ROWS, ROWS), :] = tile
    copies[0].wait()

    def split(q, s, k):
        scale = 0.5 * weights[s]
        x = buf.at[q * shots + s]
        folded = x[:, pl.ds(k, DEPTH)] * scale + x[:, pl.ds(half + k, DEPTH)] * scale
        high = folded.astype(jnp.bfloat16)
        halves[q % 2, s, pl.ds(0, LANES), pl.ds(k, DEPTH)] = high
        halves[q % 2, s, pl.ds(LANES, LANES), pl.ds(k, DEPTH)] = (folded - high.astype(jnp.float32)).astype(jnp.bfloat16)

    for s in range(shots):
        copies[1 + s].wait()
        for k in range(0, half, DEPTH):
            split(0, s, k)
    for q in range(blocks):
        if q + 1 < blocks:
            for s in range(shots):
                copies[1 + (q + 1) * shots + s].wait()
        pairs = [jnp.zeros((2 * LANES, 2 * LANES), jnp.float32)] * shots
        for k in range(0, half, DEPTH):
            for s in range(shots):
                pairs[s] += jnp.dot(
                    halves[q % 2, s, :, pl.ds(k, DEPTH)], table[pl.ds(k, DEPTH), :], preferred_element_type=jnp.float32
                )
                if q + 1 < blocks:
                    split(q + 1, s, k)
        turned = []
        for pair in pairs:
            pair = pair[:LANES] + pair[LANES:]
            turned.append((pair[:, :LANES] + pair[:, LANES:]).T)
        for g in range(HARMONICS // GROUP):
            part = slice(g * 2 * GROUP, (g + 1) * 2 * GROUP)
            block = jnp.concatenate([turned[0][part], turned[1][part]], axis=0).astype(jnp.bfloat16)
            out_refs[g // groups][pl.ds((g % groups * blocks + q) * ROWS, ROWS), :] = block


def spectra_call(frames, valid_mask):
    shots, cycles, angles = frames.shape
    blocks = cycles // LANES
    groups = HARMONICS // GROUP // CHUNKS
    rows = [groups * blocks * ROWS + (ROWS if c == 0 else 0) for c in range(CHUNKS)]
    table = jnp.asarray(half_table(angles))
    return pl.pallas_call(
        spectra_kernel,
        out_shape=[jax.ShapeDtypeStruct((r, LANES), jnp.bfloat16) for r in rows],
        in_specs=[
            pl.BlockSpec(memory_space=pltpu.SMEM),
            pl.BlockSpec(memory_space=pltpu.HBM),
            pl.BlockSpec(memory_space=pltpu.HBM),
        ],
        out_specs=[pl.BlockSpec(memory_space=pltpu.VMEM)] * CHUNKS,
        scratch_shapes=[
            pltpu.VMEM((shots * blocks, LANES, angles), jnp.float32),
            pltpu.VMEM(table.shape, jnp.bfloat16),
            pltpu.VMEM((2, shots, 2 * LANES, angles // 2), jnp.bfloat16),
            pltpu.SemaphoreType.DMA((shots * blocks + 1,)),
        ],
        compiler_params=pltpu.CompilerParams(vmem_limit_bytes=60 << 20),
        cost_estimate=pl.CostEstimate(
            flops=8 * shots * cycles * angles * LANES, bytes_accessed=frames.size * 4, transcendentals=0
        ),
        name="spectra",
    )(valid_mask, frames, table)


def correlate_kernel(tail, start_ref, *refs):
    out_ref, left, inverse = refs[-3:]
    n = left.shape[2] // ROWS
    pieces, firsts = refs[:n], refs[n : 2 * n]
    per_step = out_ref.shape[0] // GROUP
    width, cycles = out_ref.shape[1:]
    blocks = cycles // LANES
    wide = GROUP * width
    step = pl.program_id(0)

    def tiles(group, q):
        where = pl.ds(pl.multiple_of((group * blocks + q) * ROWS, ROWS), ROWS)
        return jnp.concatenate([piece[where, :] for piece in pieces], axis=0)

    @pl.when(step == 0)
    def _():
        total = jnp.zeros((ROWS // 2, LANES), jnp.float32)
        for first in firsts:
            tile = first[pl.ds(tail, ROWS), :].astype(jnp.float32)
            total += tile[: ROWS // 2] + tile[ROWS // 2 :]
        inverse[...] = 1.0 / total
        start = start_ref[0]
        lane = lax.broadcasted_iota(jnp.int32, (wide, LANES), 1)
        line = lax.broadcasted_iota(jnp.int32, (wide, LANES), 0)
        pick = jnp.where(lane == start % LANES + line % width, 1.0, 0.0).astype(jnp.bfloat16)
        lane = lax.broadcasted_iota(jnp.int32, (n * ROWS, LANES), 1)
        line = lax.broadcasted_iota(jnp.int32, (n * ROWS, LANES), 0)
        alike = jnp.where(lane % (2 * GROUP) == line % (2 * GROUP), 1.0, 0.0).astype(jnp.bfloat16)
        lane = lax.broadcasted_iota(jnp.int32, (wide, n * ROWS), 1)
        line = lax.broadcasted_iota(jnp.int32, (wide, n * ROWS), 0)
        kept = line // width == lane % (2 * GROUP) // 2
        for g in range(left.shape[0]):
            own = tiles(g, start // LANES)
            raw = lax.dot_general(pick, own, (((1,), (1,)), ((), ())), preferred_element_type=jnp.float32)
            sums = jnp.dot(raw.astype(jnp.bfloat16), alike, preferred_element_type=jnp.float32)
            mean = sums * inverse[:1, :]
            centred = raw - jnp.concatenate([mean] * (n * ROWS // LANES), axis=1)
            centred = jnp.where(kept, centred, 0.0)
            high = centred.astype(jnp.bfloat16)
            left[g, pl.ds(0, wide), :] = high
            left[g, pl.ds(wide, wide), :] = (centred - high.astype(jnp.float32)).astype(jnp.bfloat16)

    for u in range(per_step):
        group = step * per_step + u
        right = jnp.concatenate([tiles(group, q) for q in range(blocks)], axis=1)
        both = jnp.dot(left[group], right, preferred_element_type=jnp.float32)
        product = (both[:wide] + both[wide:]) * inverse[:1, :1]
        out_ref[pl.ds(u * GROUP, GROUP)] = product.reshape(GROUP, width, cycles)


def correlate_call(start, pieces, firsts, before, chunk, cycles, tail):
    n = len(pieces)
    width = cycles // n
    groups = HARMONICS // GROUP // CHUNKS
    steps = groups // 2
    operands = [start, *pieces, *firsts]
    specs = [pl.BlockSpec(memory_space=pltpu.SMEM)] + [pl.BlockSpec(memory_space=pltpu.VMEM)] * (2 * n)
    aliases = {}
    if before is not None:
        aliases = {len(operands): 0}
        operands.append(before)
        specs.append(pl.BlockSpec(memory_space=pl.ANY))
    return pl.pallas_call(
        functools.partial(correlate_kernel, tail),
        out_shape=jax.ShapeDtypeStruct((HARMONICS, width, cycles), jnp.float32),
        grid=(steps,),
        in_specs=specs,
        out_specs=pl.BlockSpec((2 * GROUP, width, cycles), lambda g: (g + chunk * steps, 0, 0)),
        scratch_shapes=[
            pltpu.VMEM((groups, 2 * GROUP * width, n * ROWS), jnp.bfloat16),
            pltpu.VMEM((ROWS // 2, LANES), jnp.float32),
        ],
        input_output_aliases=aliases,
        compiler_params=pltpu.CompilerParams(vmem_limit_bytes=24 << 20),
        cost_estimate=pl.CostEstimate(
            flops=2 * HARMONICS // CHUNKS * width * cycles * n * ROWS,
            bytes_accessed=HARMONICS // CHUNKS * width * cycles * 4,
            transcendentals=0,
        ),
        name="correlate",
    )(*operands)


def chip_at(place, chips):
    place %= chips
    if chips == 8:
        return 2 * place if place < 4 else 2 * (7 - place) + 1
    return place


def gather(piece, n, chunk):
    chips = n // 2
    place = {chip_at(p, chips): p for p in range(chips)}
    ring = {
        sign: [(i, 2 * chip_at(place[i // 2] + sign, chips) + i % 2) for i in range(n)] for sign in (1, -1)
    }
    cores = [(i, i ^ 1) for i in range(n)]
    held = [piece]
    for sign in (1, -1):
        moving = piece
        hops = chips // 2 if (sign == 1) == (chunk % 2 == 0) else chips // 2 - 1
        for _ in range(hops):
            moving = lax.ppermute(moving, "pb", ring[sign])
            held.append(moving)
    return held + [lax.ppermute(x, "pb", cores) for x in held]


def body(frames, valid_mask):
    shots, cycles, angles = frames.shape
    n = lax.axis_size("pb")
    parts = spectra_call(frames, valid_mask)
    start = (lax.axis_index("pb") * (cycles // n)).astype(jnp.int32).reshape(1)
    held = [gather(part, n, chunk) for chunk, part in enumerate(parts)]
    tail = parts[0].shape[0] - ROWS
    out = None
    for chunk in range(CHUNKS):
        out = correlate_call(start, held[chunk], held[0], out, chunk, cycles, tail)
    return out


def solution(mesh):
    placed = (P(("groups", "pb"), None, None), P(("groups", "pb")))
    return jax.shard_map(
        body, mesh=mesh, in_specs=placed, out_specs=P("groups", "pb", None), check_vma=False
    )
```

time: 65.7 us -> 51.7 us (0.79)
  waiting for transfers between devices: 20.8 us -> 15.1 us
  local copies, waits for them, and re-layouts: 5.08 us -> 0.91 us
  Pallas kernels: 16.7 us -> 13.7 us
  starting transfers between devices: 22.9 us -> 21.8 us
    ppermute x30, waiting for transfers between devices: 20.8 us -> 15.1 us  [the longest x14 15 us: gather(): moving = lax.ppermute(moving, 'pb', ring[sign])]
    unnamed x6 -> x4, local copies, waits for them, and re-layouts: 5.08 us -> 0.91 us
    pallas_call x2, Pallas kernels: 11.5 us -> 7.71 us  [correlate_call(): pl.pallas_call(functools.partial(correlate_kernel, tail), out_shape=jax.S...]
    ppermute x30, starting transfers between devices: 22.9 us -> 21.8 us  [the longest x14 19.2 us: gather(): moving = lax.ppermute(moving, 'pb', ring[sign])]
    pallas_call x1, Pallas kernels: 5.15 us -> 6 us  [spectra_call(): pl.pallas_call(spectra_kernel, out_shape=[jax.ShapeDtypeStruct((r, LANES)...]
  transfers between devices with their start and end apart: 30 -> 30, of which waited for: 10 -> 8; matrix products, arithmetic and copies ran while one was open for 0% -> 0% of each run, Pallas kernels for 8% -> 6%
where the time goes in v2:
time: 51.7 us; the launch traced here: 51.6 us
  starting transfers between devices  21.8 us (42%)
  waiting for transfers between devices  15.1 us (29%)
  Pallas kernels  13.7 us (26%)
  local copies, waits for them, and re-layouts  0.91 us (2%)
    ppermute x14, starting transfers between devices, gather(): moving = lax.ppermute(moving, 'pb', ring[sign])  19.2 us
    ppermute x14, waiting for transfers between devices, gather(): moving = lax.ppermute(moving, 'pb', ring[sign])  15 us
    pallas_call x2, Pallas kernels, correlate_call(): pl.pallas_call(functools.partial(correlate_kernel, tail), out_shape=jax.S...  7.71 us
    pallas_call x1, Pallas kernels, spectra_call(): pl.pallas_call(spectra_kernel, out_shape=[jax.ShapeDtypeStruct((r, LANES)...  6 us
    ppermute x16, starting transfers between devices, gather(): return held + [lax.ppermute(x, 'pb', cores) for x in held]  2.57 us
  transfers between devices with their start and end apart: 30, of which 8 were waited for; matrix products, arithmetic and copies ran while one was open for 0% of the time, Pallas kernels for 6%

profile of v2, /device:TPU:0, one launch (start us, length us, event | category | flops | bytes accessed | tf_op | source)
XLA Modules:
  0.0 51.6 jit_solution(2112204733999302858)
XLA Ops:
  0.0 6.0 %spectra.1 = (bf16[528,128]{1,0:T(8,128)(2,1)}, bf16[512,128]{1,0:T(8,128)(2,1)}) custom-call(s32[2]{0:T(128)} %mask_ref.1, f32[2,512,2048]{2,1,0:T(8,128)} %frames_ref.1, bf16[1024,256]{1,0:T(8,128)(2,1)} %constant.8.clone.table_ref), custom_call_target="tpu_custom_call" | custom-call | flops 2147483648 | bytes 8388608 | tf_op jit(solution)/shard_map/spectra/pallas_call | solution.py:94
  6.0 3.1 %collective-permute-start.15 = (bf16[528,128]{1,0:T(8,128)(2,1)}, bf16[528,128]{1,0:T(8,128)(2,1)S(1)}, u32[]{:S(2)}, u32[]{:S(2)}) collective-permute-start(bf16[528,128]{1,0:T(8,128)(2,1)} %get-tuple-element.8.refs_0_.refs_16_), channel_id=1, source_target_pairs={{0,4},{1,5},{2,0},{3,1},{4,8},{5,9},{6,2},{7,3},{8,12},{9,13},{10,... | collective-permute-start | bytes 405512 | tf_op jit(solution)/shard_map/ppermute | solution.py:219
  9.1 0.0 collective-permute-start.7
  9.1 0.5 collective-permute-start.22
  9.6 0.0 collective-permute-start.3
  9.6 2.0 %collective-permute-start = (bf16[512,128]{1,0:T(8,128)(2,1)}, bf16[512,128]{1,0:T(8,128)(2,1)S(1)}, u32[]{:S(2)}, u32[]{:S(2)}) collective-permute-start(bf16[512,128]{1,0:T(8,128)(2,1)} %get-tuple-element.7.refs_0_), channel_id=1, source_target_pairs={{0,4},{1,5},{2,0},{3,1},{4,8},{5,9},{6,2},{7,3},{8,12},{9,13},{10,... | collective-permute-start | bytes 393224 | tf_op jit(solution)/shard_map/ppermute | solution.py:219
  11.6 0.0 collective-permute-done.7.refs_8_
  11.6 0.0 collective-permute-start.19
  11.7 1.6 %collective-permute-done.15.refs_1_.refs_17_ = bf16[528,128]{1,0:T(8,128)(2,1)S(1)} collective-permute-done((bf16[528,128]{1,0:T(8,128)(2,1)}, bf16[528,128]{1,0:T(8,128)(2,1)S(1)}, u32[]{:S(2)}, u32[]{:S(2)}) %collective-permute-start.15) | collective-permute-done | bytes 135200 | tf_op jit(solution)/shard_map/ppermute | solution.py:219
  13.2 1.9 %collective-permute-start.16 = (bf16[528,128]{1,0:T(8,128)(2,1)S(1)}, bf16[528,128]{1,0:T(8,128)(2,1)S(1)}, u32[]{:S(2)}, u32[]{:S(2)}) collective-permute-start(bf16[528,128]{1,0:T(8,128)(2,1)S(1)} %collective-permute-done.15.refs_1_.refs_17_), channel_id=1, source_target_pairs={{0,4},{1,5},{2,0},{3,1},{4,8},{5,9},{6,2},{7,3},{8,12},{9,13},{10,... | collective-permute-start | bytes 405512 | tf_op jit(solution)/shard_map/ppermute | solution.py:219
  15.1 1.1 %collective-permute-done.3.refs_4_ = bf16[512,128]{1,0:T(8,128)(2,1)S(1)} collective-permute-done((bf16[512,128]{1,0:T(8,128)(2,1)}, bf16[512,128]{1,0:T(8,128)(2,1)S(1)}, u32[]{:S(2)}, u32[]{:S(2)}) %collective-permute-start.3) | collective-permute-done | bytes 131104 | tf_op jit(solution)/shard_map/ppermute | solution.py:219
  16.2 0.0 collective-permute-start.11
  16.2 0.0 collective-permute-done.refs_1_
  16.2 1.9 %collective-permute-start.4 = (bf16[512,128]{1,0:T(8,128)(2,1)S(1)}, bf16[512,128]{1,0:T(8,128)(2,1)S(1)}, u32[]{:S(2)}, u32[]{:S(2)}) collective-permute-start(bf16[512,128]{1,0:T(8,128)(2,1)S(1)} %collective-permute-done.3.refs_4_), channel_id=1, source_target_pairs={{0,2},{1,3},{2,6},{3,7},{4,0},{5,1},{6,10},{7,11},{8,4},{9,5},{10,... | collective-permute-start | bytes 393224 | tf_op jit(solution)/shard_map/ppermute | solution.py:219
  18.2 0.0 collective-permute-done.22.refs_8_.refs_24_
  18.2 0.0 collective-permute-start.8
  18.2 1.6 %collective-permute-start.20 = (bf16[528,128]{1,0:T(8,128)(2,1)S(1)}, bf16[528,128]{1,0:T(8,128)(2,1)S(1)}, u32[]{:S(2)}, u32[]{:S(2)}) collective-permute-start(bf16[528,128]{1,0:T(8,128)(2,1)S(1)} %collective-permute-done.19.refs_5_.refs_21_), channel_id=1, source_target_pairs={{0,2},{1,3},{2,6},{3,7},{4,0},{5,1},{6,10},{7,11},{8,4},{9,5},{10,... | collective-permute-start | bytes 405512 | tf_op jit(solution)/shard_map/ppermute | solution.py:219
  19.8 0.0 collective-permute-done.16.refs_2_.refs_18_
  19.8 0.5 %collective-permute-start.17 = (bf16[528,128]{1,0:T(8,128)(2,1)S(1)}, bf16[528,128]{1,0:T(8,128)(2,1)S(1)}, u32[]{:S(2)}, u32[]{:S(2)}) collective-permute-start(bf16[528,128]{1,0:T(8,128)(2,1)S(1)} %collective-permute-done.16.refs_2_.refs_18_), channel_id=1, source_target_pairs={{0,4},{1,5},{2,0},{3,1},{4,8},{5,9},{6,2},{7,3},{8,12},{9,13},{10,... | collective-permute-start | bytes 405512 | tf_op jit(solution)/shard_map/ppermute | solution.py:219
  20.4 2.2 %collective-permute-done.4.refs_5_ = bf16[512,128]{1,0:T(8,128)(2,1)S(1)} collective-permute-done((bf16[512,128]{1,0:T(8,128)(2,1)S(1)}, bf16[512,128]{1,0:T(8,128)(2,1)S(1)}, u32[]{:S(2)}, u32[]{:S(2)}) %collective-permute-start.4) | collective-permute-done | bytes 131104 | tf_op jit(solution)/shard_map/ppermute | solution.py:219
  22.6 0.0 collective-permute-start.23
  22.6 0.0 collective-permute-done.8.refs_9_
  22.6 2.0 %collective-permute-start.1 = (bf16[512,128]{1,0:T(8,128)(2,1)S(1)}, bf16[512,128]{1,0:T(8,128)(2,1)S(1)}, u32[]{:S(2)}, u32[]{:S(2)}) collective-permute-start(bf16[512,128]{1,0:T(8,128)(2,1)S(1)} %collective-permute-done.refs_1_), channel_id=1, source_target_pairs={{0,4},{1,5},{2,0},{3,1},{4,8},{5,9},{6,2},{7,3},{8,12},{9,13},{10,... | collective-permute-start | bytes 393224 | tf_op jit(solution)/shard_map/ppermute | solution.py:219
  24.6 0.4 collective-permute-done.20.refs_6_.refs_22_
  25.0 1.0 %collective-permute-start.21 = (bf16[528,128]{1,0:T(8,128)(2,1)S(1)}, bf16[528,128]{1,0:T(8,128)(2,1)S(1)}, u32[]{:S(2)}, u32[]{:S(2)}) collective-permute-start(bf16[528,128]{1,0:T(8,128)(2,1)S(1)} %collective-permute-done.20.refs_6_.refs_22_), channel_id=1, source_target_pairs={{0,2},{1,3},{2,6},{3,7},{4,0},{5,1},{6,10},{7,11},{8,4},{9,5},{10,... | collective-permute-start | bytes 405512 | tf_op jit(solution)/shard_map/ppermute | solution.py:219
  26.0 0.0 collective-permute-done.17.refs_3_.refs_19_
  26.0 1.0 %collective-permute-start.18 = (bf16[528,128]{1,0:T(8,128)(2,1)S(1)}, bf16[528,128]{1,0:T(8,128)(2,1)S(1)}, u32[]{:S(2)}, u32[]{:S(2)}) collective-permute-start(bf16[528,128]{1,0:T(8,128)(2,1)S(1)} %collective-permute-done.17.refs_3_.refs_19_), channel_id=1, source_target_pairs={{0,4},{1,5},{2,0},{3,1},{4,8},{5,9},{6,2},{7,3},{8,12},{9,13},{10,... | collective-permute-start | bytes 405512 | tf_op jit(solution)/shard_map/ppermute | solution.py:219
  27.0 1.8 %collective-permute-done.1.refs_2_ = bf16[512,128]{1,0:T(8,128)(2,1)S(1)} collective-permute-done((bf16[512,128]{1,0:T(8,128)(2,1)S(1)}, bf16[512,128]{1,0:T(8,128)(2,1)S(1)}, u32[]{:S(2)}, u32[]{:S(2)}) %collective-permute-start.1) | collective-permute-done | bytes 131104 | tf_op jit(solution)/shard_map/ppermute | solution.py:219
  28.8 1.1 %collective-permute-start.5 = (bf16[512,128]{1,0:T(8,128)(2,1)S(1)}, bf16[512,128]{1,0:T(8,128)(2,1)S(1)}, u32[]{:S(2)}, u32[]{:S(2)}) collective-permute-start(bf16[512,128]{1,0:T(8,128)(2,1)S(1)} %collective-permute-done.4.refs_5_), channel_id=1, source_target_pairs={{0,2},{1,3},{2,6},{3,7},{4,0},{5,1},{6,10},{7,11},{8,4},{9,5},{10,... | collective-permute-start | bytes 393224 | tf_op jit(solution)/shard_map/ppermute | solution.py:219
  30.0 0.0 collective-permute-done.27.refs_13_.refs_29_
  30.0 1.1 %collective-permute-start.2 = (bf16[512,128]{1,0:T(8,128)(2,1)S(1)}, bf16[512,128]{1,0:T(8,128)(2,1)S(1)}, u32[]{:S(2)}, u32[]{:S(2)}) collective-permute-start(bf16[512,128]{1,0:T(8,128)(2,1)S(1)} %collective-permute-done.1.refs_2_), channel_id=1, source_target_pairs={{0,4},{1,5},{2,0},{3,1},{4,8},{5,9},{6,2},{7,3},{8,12},{9,13},{10,... | collective-permute-start | bytes 393224 | tf_op jit(solution)/shard_map/ppermute | solution.py:219
  31.0 2.9 %collective-permute-done.5.refs_6_ = bf16[512,128]{1,0:T(8,128)(2,1)S(1)} collective-permute-done((bf16[512,128]{1,0:T(8,128)(2,1)S(1)}, bf16[512,128]{1,0:T(8,128)(2,1)S(1)}, u32[]{:S(2)}, u32[]{:S(2)}) %collective-permute-start.5) | collective-permute-done | bytes 131104 | tf_op jit(solution)/shard_map/ppermute | solution.py:219
  33.9 0.0 collective-permute-start.24
  33.9 0.0 collective-permute-done.21.refs_7_.refs_23_
  33.9 0.5 collective-permute-start.29
  34.4 1.5 %collective-permute-done.2.refs_3_ = bf16[512,128]{1,0:T(8,128)(2,1)S(1)} collective-permute-done((bf16[512,128]{1,0:T(8,128)(2,1)S(1)}, bf16[512,128]{1,0:T(8,128)(2,1)S(1)}, u32[]{:S(2)}, u32[]{:S(2)}) %collective-permute-start.2) | collective-permute-done | bytes 131104 | tf_op jit(solution)/shard_map/ppermute | solution.py:219
  35.9 0.0 collective-permute-start.25
  35.9 0.0 collective-permute-done.18.refs_4_.refs_20_
  35.9 0.5 collective-permute-start.26
  36.4 0.0 collective-permute-done.28.refs_14_.refs_30_
  36.4 1.9 %collective-permute-start.6 = (bf16[512,128]{1,0:T(8,128)(2,1)S(1)}, bf16[512,128]{1,0:T(8,128)(2,1)S(1)}, u32[]{:S(2)}, u32[]{:S(2)}) collective-permute-start(bf16[512,128]{1,0:T(8,128)(2,1)S(1)} %collective-permute-done.5.refs_6_), channel_id=1, source_target_pairs={{0,2},{1,3},{2,6},{3,7},{4,0},{5,1},{6,10},{7,11},{8,4},{9,5},{10,... | collective-permute-start | bytes 393224 | tf_op jit(solution)/shard_map/ppermute | solution.py:219
  38.3 3.6 %collective-permute-done.6.refs_7_ = bf16[512,128]{1,0:T(8,128)(2,1)S(1)} collective-permute-done((bf16[512,128]{1,0:T(8,128)(2,1)S(1)}, bf16[512,128]{1,0:T(8,128)(2,1)S(1)}, u32[]{:S(2)}, u32[]{:S(2)}) %collective-permute-start.6) | collective-permute-done | bytes 131104 | tf_op jit(solution)/shard_map/ppermute | solution.py:219
  41.9 0.5 collective-permute-start.13
  42.4 0.1 collective-permute-start.10
  42.5 0.4 collective-permute-start.14
  42.9 0.9 %copy-done = bf16[528,128]{1,0:T(8,128)(2,1)S(1)} copy-done((bf16[528,128]{1,0:T(8,128)(2,1)S(1)}, bf16[528,128]{1,0:T(8,128)(2,1)}, u32[]{:S(2)}) %copy-start) | copy-done | bytes 135192
  43.8 3.3 %correlate.2.refs_32_ = f32[64,32,512]{2,1,0:T(8,128)} custom-call(s32[1]{0:T(128)} %bitcast.start_ref, bf16[528,128]{1,0:T(8,128)(2,1)S(1)} %copy-done, bf16[528,128]{1,0:T(8,128)(2,1)S(1)} %collective-permute-done.15.refs_1_.refs_17_, bf16[528,128]{1,0:T(8,128)(2,1)S(1)} %collective-permute-done.16.refs_2_.refs_18_, ...), custom_call_target="tpu_custom_call" | custom-call | flops 268435456 | bytes 2097152 | tf_op jit(solution)/shard_map/correlate/pallas_call | solution.py:179
  47.1 4.5 %correlate.3 = f32[64,32,512]{2,1,0:T(8,128)} custom-call(s32[1]{0:T(128)} %bitcast.start_ref, bf16[512,128]{1,0:T(8,128)(2,1)S(1)} %copy-done.1, bf16[512,128]{1,0:T(8,128)(2,1)S(1)} %collective-permute-done.refs_1_, bf16[512,128]{1,0:T(8,128)(2,1)S(1)} %collective-permute-done.1.refs_2_, ...), custom_call_target="tpu_custom_call", output_to_operand_aliasing={{}: (33, {})} | custom-call | flops 268435456 | bytes 2097152 | tf_op jit(solution)/shard_map/correlate/pallas_call | solution.py:179
  (19 shorter events, 0.0 us)
Async XLA Ops:
  6.0 7.2 %collective-permute-start.15 = (bf16[528,128]{1,0:T(8,128)(2,1)}, bf16[528,128]{1,0:T(8,128)(2,1)S(1)}, u32[]{:S(2)}, u32[]{:S(2)}) collective-permute-start(bf16[528,128]{1,0:T(8,128)(2,1)} %get-tuple-element.8.refs_0_.refs_16_), channel_id=1, source_target_pairs={{0,4},{1,5},{2,0},{3,1},{4,8},{5,9},{6,2},{7,3},{8,12},{9,13},{10,... | collective-permute-start | bytes 405512 | tf_op jit(solution)/shard_map/ppermute | solution.py:219
  9.1 2.5 %collective-permute-start.7 = (bf16[512,128]{1,0:T(8,128)(2,1)}, bf16[512,128]{1,0:T(8,128)(2,1)S(1)}, u32[]{:S(2)}, u32[]{:S(2)}) collective-permute-start(bf16[512,128]{1,0:T(8,128)(2,1)} %get-tuple-element.7.refs_0_), channel_id=1, source_target_pairs={{0,1},{1,0},{2,3},{3,2},{4,5},{5,4},{6,7},{7,6},{8,9},{9,8},{10,11... | collective-permute-start | bytes 393224 | tf_op jit(solution)/shard_map/ppermute | solution.py:221
  9.1 9.1 %collective-permute-start.22 = (bf16[528,128]{1,0:T(8,128)(2,1)}, bf16[528,128]{1,0:T(8,128)(2,1)S(1)}, u32[]{:S(2)}, u32[]{:S(2)}) collective-permute-start(bf16[528,128]{1,0:T(8,128)(2,1)} %get-tuple-element.8.refs_0_.refs_16_), channel_id=1, source_target_pairs={{0,1},{1,0},{2,3},{3,2},{4,5},{5,4},{6,7},{7,6},{8,9},{9,8},{10,11... | collective-permute-start | bytes 405512 | tf_op jit(solution)/shard_map/ppermute | solution.py:221
  9.6 6.6 %collective-permute-start.3 = (bf16[512,128]{1,0:T(8,128)(2,1)}, bf16[512,128]{1,0:T(8,128)(2,1)S(1)}, u32[]{:S(2)}, u32[]{:S(2)}) collective-permute-start(bf16[512,128]{1,0:T(8,128)(2,1)} %get-tuple-element.7.refs_0_), channel_id=1, source_target_pairs={{0,2},{1,3},{2,6},{3,7},{4,0},{5,1},{6,10},{7,11},{8,4},{9,5},{10,... | collective-permute-start | bytes 393224 | tf_op jit(solution)/shard_map/ppermute | solution.py:219
  9.6 6.6 %collective-permute-start = (bf16[512,128]{1,0:T(8,128)(2,1)}, bf16[512,128]{1,0:T(8,128)(2,1)S(1)}, u32[]{:S(2)}, u32[]{:S(2)}) collective-permute-start(bf16[512,128]{1,0:T(8,128)(2,1)} %get-tuple-element.7.refs_0_), channel_id=1, source_target_pairs={{0,4},{1,5},{2,0},{3,1},{4,8},{5,9},{6,2},{7,3},{8,12},{9,13},{10,... | collective-permute-start | bytes 393224 | tf_op jit(solution)/shard_map/ppermute | solution.py:219
  11.6 6.5 %collective-permute-start.19 = (bf16[528,128]{1,0:T(8,128)(2,1)}, bf16[528,128]{1,0:T(8,128)(2,1)S(1)}, u32[]{:S(2)}, u32[]{:S(2)}) collective-permute-start(bf16[528,128]{1,0:T(8,128)(2,1)} %get-tuple-element.8.refs_0_.refs_16_), channel_id=1, source_target_pairs={{0,2},{1,3},{2,6},{3,7},{4,0},{5,1},{6,10},{7,11},{8,4},{9,5},{10,... | collective-permute-start | bytes 405512 | tf_op jit(solution)/shard_map/ppermute | solution.py:219
  13.2 6.6 %collective-permute-start.16 = (bf16[528,128]{1,0:T(8,128)(2,1)S(1)}, bf16[528,128]{1,0:T(8,128)(2,1)S(1)}, u32[]{:S(2)}, u32[]{:S(2)}) collective-permute-start(bf16[528,128]{1,0:T(8,128)(2,1)S(1)} %collective-permute-done.15.refs_1_.refs_17_), channel_id=1, source_target_pairs={{0,4},{1,5},{2,0},{3,1},{4,8},{5,9},{6,2},{7,3},{8,12},{9,13},{10,... | collective-permute-start | bytes 405512 | tf_op jit(solution)/shard_map/ppermute | solution.py:219
  16.2 4.2 %collective-permute-start.11 = (bf16[512,128]{1,0:T(8,128)(2,1)S(1)}, bf16[512,128]{1,0:T(8,128)(2,1)S(1)}, u32[]{:S(2)}, u32[]{:S(2)}) collective-permute-start(bf16[512,128]{1,0:T(8,128)(2,1)S(1)} %collective-permute-done.3.refs_4_), channel_id=1, source_target_pairs={{0,1},{1,0},{2,3},{3,2},{4,5},{5,4},{6,7},{7,6},{8,9},{9,8},{10,11... | collective-permute-start | bytes 393224 | tf_op jit(solution)/shard_map/ppermute | solution.py:221
  16.2 6.4 %collective-permute-start.4 = (bf16[512,128]{1,0:T(8,128)(2,1)S(1)}, bf16[512,128]{1,0:T(8,128)(2,1)S(1)}, u32[]{:S(2)}, u32[]{:S(2)}) collective-permute-start(bf16[512,128]{1,0:T(8,128)(2,1)S(1)} %collective-permute-done.3.refs_4_), channel_id=1, source_target_pairs={{0,2},{1,3},{2,6},{3,7},{4,0},{5,1},{6,10},{7,11},{8,4},{9,5},{10,... | collective-permute-start | bytes 393224 | tf_op jit(solution)/shard_map/ppermute | solution.py:219
  18.2 4.4 %collective-permute-start.8 = (bf16[512,128]{1,0:T(8,128)(2,1)S(1)}, bf16[512,128]{1,0:T(8,128)(2,1)S(1)}, u32[]{:S(2)}, u32[]{:S(2)}) collective-permute-start(bf16[512,128]{1,0:T(8,128)(2,1)S(1)} %collective-permute-done.refs_1_), channel_id=1, source_target_pairs={{0,1},{1,0},{2,3},{3,2},{4,5},{5,4},{6,7},{7,6},{8,9},{9,8},{10,11... | collective-permute-start | bytes 393224 | tf_op jit(solution)/shard_map/ppermute | solution.py:221
  18.2 6.8 %collective-permute-start.20 = (bf16[528,128]{1,0:T(8,128)(2,1)S(1)}, bf16[528,128]{1,0:T(8,128)(2,1)S(1)}, u32[]{:S(2)}, u32[]{:S(2)}) collective-permute-start(bf16[528,128]{1,0:T(8,128)(2,1)S(1)} %collective-permute-done.19.refs_5_.refs_21_), channel_id=1, source_target_pairs={{0,2},{1,3},{2,6},{3,7},{4,0},{5,1},{6,10},{7,11},{8,4},{9,5},{10,... | collective-permute-start | bytes 405512 | tf_op jit(solution)/shard_map/ppermute | solution.py:219
  19.8 6.2 %collective-permute-start.17 = (bf16[528,128]{1,0:T(8,128)(2,1)S(1)}, bf16[528,128]{1,0:T(8,128)(2,1)S(1)}, u32[]{:S(2)}, u32[]{:S(2)}) collective-permute-start(bf16[528,128]{1,0:T(8,128)(2,1)S(1)} %collective-permute-done.16.refs_2_.refs_18_), channel_id=1, source_target_pairs={{0,4},{1,5},{2,0},{3,1},{4,8},{5,9},{6,2},{7,3},{8,12},{9,13},{10,... | collective-permute-start | bytes 405512 | tf_op jit(solution)/shard_map/ppermute | solution.py:219
  20.4 9.6 %collective-permute-start.27 = (bf16[528,128]{1,0:T(8,128)(2,1)S(1)}, bf16[528,128]{1,0:T(8,128)(2,1)S(1)}, u32[]{:S(2)}, u32[]{:S(2)}) collective-permute-start(bf16[528,128]{1,0:T(8,128)(2,1)S(1)} %collective-permute-done.19.refs_5_.refs_21_), channel_id=1, source_target_pairs={{0,1},{1,0},{2,3},{3,2},{4,5},{5,4},{6,7},{7,6},{8,9},{9,8},{10,11... | collective-permute-start | bytes 405512 | tf_op jit(solution)/shard_map/ppermute | solution.py:221
  22.6 7.4 %collective-permute-start.23 = (bf16[528,128]{1,0:T(8,128)(2,1)S(1)}, bf16[528,128]{1,0:T(8,128)(2,1)S(1)}, u32[]{:S(2)}, u32[]{:S(2)}) collective-permute-start(bf16[528,128]{1,0:T(8,128)(2,1)S(1)} %collective-permute-done.15.refs_1_.refs_17_), channel_id=1, source_target_pairs={{0,1},{1,0},{2,3},{3,2},{4,5},{5,4},{6,7},{7,6},{8,9},{9,8},{10,11... | collective-permute-start | bytes 405512 | tf_op jit(solution)/shard_map/ppermute | solution.py:221
  22.6 6.2 %collective-permute-start.1 = (bf16[512,128]{1,0:T(8,128)(2,1)S(1)}, bf16[512,128]{1,0:T(8,128)(2,1)S(1)}, u32[]{:S(2)}, u32[]{:S(2)}) collective-permute-start(bf16[512,128]{1,0:T(8,128)(2,1)S(1)} %collective-permute-done.refs_1_), channel_id=1, source_target_pairs={{0,4},{1,5},{2,0},{3,1},{4,8},{5,9},{6,2},{7,3},{8,12},{9,13},{10,... | collective-permute-start | bytes 393224 | tf_op jit(solution)/shard_map/ppermute | solution.py:219
  25.0 8.9 %collective-permute-start.21 = (bf16[528,128]{1,0:T(8,128)(2,1)S(1)}, bf16[528,128]{1,0:T(8,128)(2,1)S(1)}, u32[]{:S(2)}, u32[]{:S(2)}) collective-permute-start(bf16[528,128]{1,0:T(8,128)(2,1)S(1)} %collective-permute-done.20.refs_6_.refs_22_), channel_id=1, source_target_pairs={{0,2},{1,3},{2,6},{3,7},{4,0},{5,1},{6,10},{7,11},{8,4},{9,5},{10,... | collective-permute-start | bytes 405512 | tf_op jit(solution)/shard_map/ppermute | solution.py:219
  26.0 9.9 %collective-permute-start.18 = (bf16[528,128]{1,0:T(8,128)(2,1)S(1)}, bf16[528,128]{1,0:T(8,128)(2,1)S(1)}, u32[]{:S(2)}, u32[]{:S(2)}) collective-permute-start(bf16[528,128]{1,0:T(8,128)(2,1)S(1)} %collective-permute-done.17.refs_3_.refs_19_), channel_id=1, source_target_pairs={{0,4},{1,5},{2,0},{3,1},{4,8},{5,9},{6,2},{7,3},{8,12},{9,13},{10,... | collective-permute-start | bytes 405512 | tf_op jit(solution)/shard_map/ppermute | solution.py:219
  28.8 5.1 %collective-permute-start.5 = (bf16[512,128]{1,0:T(8,128)(2,1)S(1)}, bf16[512,128]{1,0:T(8,128)(2,1)S(1)}, u32[]{:S(2)}, u32[]{:S(2)}) collective-permute-start(bf16[512,128]{1,0:T(8,128)(2,1)S(1)} %collective-permute-done.4.refs_5_), channel_id=1, source_target_pairs={{0,2},{1,3},{2,6},{3,7},{4,0},{5,1},{6,10},{7,11},{8,4},{9,5},{10,... | collective-permute-start | bytes 393224 | tf_op jit(solution)/shard_map/ppermute | solution.py:219
  30.0 6.4 %collective-permute-start.28 = (bf16[528,128]{1,0:T(8,128)(2,1)S(1)}, bf16[528,128]{1,0:T(8,128)(2,1)S(1)}, u32[]{:S(2)}, u32[]{:S(2)}) collective-permute-start(bf16[528,128]{1,0:T(8,128)(2,1)S(1)} %collective-permute-done.20.refs_6_.refs_22_), channel_id=1, source_target_pairs={{0,1},{1,0},{2,3},{3,2},{4,5},{5,4},{6,7},{7,6},{8,9},{9,8},{10,11... | collective-permute-start | bytes 405512 | tf_op jit(solution)/shard_map/ppermute | solution.py:221
  30.0 5.9 %collective-permute-start.2 = (bf16[512,128]{1,0:T(8,128)(2,1)S(1)}, bf16[512,128]{1,0:T(8,128)(2,1)S(1)}, u32[]{:S(2)}, u32[]{:S(2)}) collective-permute-start(bf16[512,128]{1,0:T(8,128)(2,1)S(1)} %collective-permute-done.1.refs_2_), channel_id=1, source_target_pairs={{0,4},{1,5},{2,0},{3,1},{4,8},{5,9},{6,2},{7,3},{8,12},{9,13},{10,... | collective-permute-start | bytes 393224 | tf_op jit(solution)/shard_map/ppermute | solution.py:219
  33.9 4.4 %collective-permute-start.24 = (bf16[528,128]{1,0:T(8,128)(2,1)S(1)}, bf16[528,128]{1,0:T(8,128)(2,1)S(1)}, u32[]{:S(2)}, u32[]{:S(2)}) collective-permute-start(bf16[528,128]{1,0:T(8,128)(2,1)S(1)} %collective-permute-done.16.refs_2_.refs_18_), channel_id=1, source_target_pairs={{0,1},{1,0},{2,3},{3,2},{4,5},{5,4},{6,7},{7,6},{8,9},{9,8},{10,11... | collective-permute-start | bytes 405512 | tf_op jit(solution)/shard_map/ppermute | solution.py:221
  33.9 7.9 %collective-permute-start.29 = (bf16[528,128]{1,0:T(8,128)(2,1)S(1)}, bf16[528,128]{1,0:T(8,128)(2,1)S(1)}, u32[]{:S(2)}, u32[]{:S(2)}) collective-permute-start(bf16[528,128]{1,0:T(8,128)(2,1)S(1)} %collective-permute-done.21.refs_7_.refs_23_), channel_id=1, source_target_pairs={{0,1},{1,0},{2,3},{3,2},{4,5},{5,4},{6,7},{7,6},{8,9},{9,8},{10,11... | collective-permute-start | bytes 405512 | tf_op jit(solution)/shard_map/ppermute | solution.py:221
  35.9 6.5 %collective-permute-start.25 = (bf16[528,128]{1,0:T(8,128)(2,1)S(1)}, bf16[528,128]{1,0:T(8,128)(2,1)S(1)}, u32[]{:S(2)}, u32[]{:S(2)}) collective-permute-start(bf16[528,128]{1,0:T(8,128)(2,1)S(1)} %collective-permute-done.17.refs_3_.refs_19_), channel_id=1, source_target_pairs={{0,1},{1,0},{2,3},{3,2},{4,5},{5,4},{6,7},{7,6},{8,9},{9,8},{10,11... | collective-permute-start | bytes 405512 | tf_op jit(solution)/shard_map/ppermute | solution.py:221
  35.9 6.6 %collective-permute-start.26 = (bf16[528,128]{1,0:T(8,128)(2,1)S(1)}, bf16[528,128]{1,0:T(8,128)(2,1)S(1)}, u32[]{:S(2)}, u32[]{:S(2)}) collective-permute-start(bf16[528,128]{1,0:T(8,128)(2,1)S(1)} %collective-permute-done.18.refs_4_.refs_20_), channel_id=1, source_target_pairs={{0,1},{1,0},{2,3},{3,2},{4,5},{5,4},{6,7},{7,6},{8,9},{9,8},{10,11... | collective-permute-start | bytes 405512 | tf_op jit(solution)/shard_map/ppermute | solution.py:221
  36.4 5.5 %collective-permute-start.6 = (bf16[512,128]{1,0:T(8,128)(2,1)S(1)}, bf16[512,128]{1,0:T(8,128)(2,1)S(1)}, u32[]{:S(2)}, u32[]{:S(2)}) collective-permute-start(bf16[512,128]{1,0:T(8,128)(2,1)S(1)} %collective-permute-done.5.refs_6_), channel_id=1, source_target_pairs={{0,2},{1,3},{2,6},{3,7},{4,0},{5,1},{6,10},{7,11},{8,4},{9,5},{10,... | collective-permute-start | bytes 393224 | tf_op jit(solution)/shard_map/ppermute | solution.py:219
  38.3 8.8 %collective-permute-start.12 = (bf16[512,128]{1,0:T(8,128)(2,1)S(1)}, bf16[512,128]{1,0:T(8,128)(2,1)S(1)}, u32[]{:S(2)}, u32[]{:S(2)}) collective-permute-start(bf16[512,128]{1,0:T(8,128)(2,1)S(1)} %collective-permute-done.4.refs_5_), channel_id=1, source_target_pairs={{0,1},{1,0},{2,3},{3,2},{4,5},{5,4},{6,7},{7,6},{8,9},{9,8},{10,11... | collective-permute-start | bytes 393224 | tf_op jit(solution)/shard_map/ppermute | solution.py:221
  41.9 5.2 %collective-permute-start.9 = (bf16[512,128]{1,0:T(8,128)(2,1)S(1)}, bf16[512,128]{1,0:T(8,128)(2,1)}, u32[]{:S(2)}, u32[]{:S(2)}) collective-permute-start(bf16[512,128]{1,0:T(8,128)(2,1)S(1)} %collective-permute-done.1.refs_2_), channel_id=1, source_target_pairs={{0,1},{1,0},{2,3},{3,2},{4,5},{5,4},{6,7},{7,6},{8,9},{9,8},{10,11... | collective-permute-start | bytes 393224 | tf_op jit(solution)/shard_map/ppermute | solution.py:221
  41.9 5.2 %collective-permute-start.13 = (bf16[512,128]{1,0:T(8,128)(2,1)S(1)}, bf16[512,128]{1,0:T(8,128)(2,1)}, u32[]{:S(2)}, u32[]{:S(2)}) collective-permute-start(bf16[512,128]{1,0:T(8,128)(2,1)S(1)} %collective-permute-done.5.refs_6_), channel_id=1, source_target_pairs={{0,1},{1,0},{2,3},{3,2},{4,5},{5,4},{6,7},{7,6},{8,9},{9,8},{10,11... | collective-permute-start | bytes 393224 | tf_op jit(solution)/shard_map/ppermute | solution.py:221
  42.4 4.7 %collective-permute-start.10 = (bf16[512,128]{1,0:T(8,128)(2,1)S(1)}, bf16[512,128]{1,0:T(8,128)(2,1)}, u32[]{:S(2)}, u32[]{:S(2)}) collective-permute-start(bf16[512,128]{1,0:T(8,128)(2,1)S(1)} %collective-permute-done.2.refs_3_), channel_id=1, source_target_pairs={{0,1},{1,0},{2,3},{3,2},{4,5},{5,4},{6,7},{7,6},{8,9},{9,8},{10,11... | collective-permute-start | bytes 393224 | tf_op jit(solution)/shard_map/ppermute | solution.py:221
  42.5 4.6 %collective-permute-start.14 = (bf16[512,128]{1,0:T(8,128)(2,1)S(1)}, bf16[512,128]{1,0:T(8,128)(2,1)}, u32[]{:S(2)}, u32[]{:S(2)}) collective-permute-start(bf16[512,128]{1,0:T(8,128)(2,1)S(1)} %collective-permute-done.6.refs_7_), channel_id=1, source_target_pairs={{0,1},{1,0},{2,3},{3,2},{4,5},{5,4},{6,7},{7,6},{8,9},{9,8},{10,11... | collective-permute-start | bytes 393224 | tf_op jit(solution)/shard_map/ppermute | solution.py:221
  42.9 0.9 %copy-start = (bf16[528,128]{1,0:T(8,128)(2,1)S(1)}, bf16[528,128]{1,0:T(8,128)(2,1)}, u32[]{:S(2)}) copy-start(bf16[528,128]{1,0:T(8,128)(2,1)} %get-tuple-element.8.refs_0_.refs_16_) | copy-start | bytes 405508
  43.8 3.3 %copy-start.1 = (bf16[512,128]{1,0:T(8,128)(2,1)S(1)}, bf16[512,128]{1,0:T(8,128)(2,1)}, u32[]{:S(2)}) copy-start(bf16[512,128]{1,0:T(8,128)(2,1)} %get-tuple-element.7.refs_0_) | copy-start | bytes 393220

commit v3 on v2

--- a/solution.py
+++ b/solution.py
@@ -1,4 +1,3 @@
-import functools
 import math
 
 import jax
@@ -14,11 +13,12 @@
 GROUP = 4
 ROWS = 4 * GROUP
 CHUNKS = 2
+PAD = 8
 DEPTH = 256
 
 
-def half_table(angles):
-    order = 2 * (np.arange(HARMONICS) + 1)
+def half_table(angles, first):
+    order = 2 * ((np.arange(HARMONICS) + first) % HARMONICS + 1)
     wrapped = np.arange(angles // 2)[:, None] * order[None, :] % angles
     phase = wrapped * (2.0 * math.pi / angles)
     table = np.stack([np.cos(phase), -np.sin(phase)], axis=-1).reshape(angles // 2, 2 * HARMONICS)
@@ -28,14 +28,14 @@
     return np.concatenate([high, low], axis=1)
 
 
-def spectra_kernel(mask_ref, frames_ref, table_ref, *refs):
+def spectra_kernel(mask_ref, core_ref, frames_ref, table_ref, *refs):
     out_refs = refs[:CHUNKS]
     buf, table, halves, sems = refs[CHUNKS:]
     shots, cycles, angles = frames_ref.shape
     blocks = cycles // LANES
     half = angles // 2
     groups = HARMONICS // GROUP // CHUNKS
-    copies = [pltpu.make_async_copy(table_ref, table, sems.at[shots * blocks])]
+    copies = [pltpu.make_async_copy(table_ref.at[core_ref[0]], table, sems.at[shots * blocks])]
     for q in range(blocks):
         for s in range(shots):
             copies.append(
@@ -46,9 +46,9 @@
     for copy in copies:
         copy.start()
     weights = [mask_ref[s].astype(jnp.float32) for s in range(shots)]
-    row = lax.broadcasted_iota(jnp.int32, (ROWS, LANES), 0)
-    tile = jnp.where(row < ROWS // 2, weights[0], weights[1]).astype(jnp.bfloat16)
-    out_refs[0][pl.ds(groups * blocks * ROWS, ROWS), :] = tile
+    count = jnp.full((PAD, LANES), weights[0] + weights[1], jnp.float32).astype(jnp.bfloat16)
+    for out_ref in out_refs:
+        out_ref[pl.ds(groups * blocks * ROWS, PAD), :] = count
     copies[0].wait()
 
     def split(q, s, k):
@@ -85,16 +85,17 @@
             out_refs[g // groups][pl.ds((g % groups * blocks + q) * ROWS, ROWS), :] = block
 
 
-def spectra_call(frames, valid_mask):
+def spectra_call(frames, valid_mask, core):
     shots, cycles, angles = frames.shape
     blocks = cycles // LANES
     groups = HARMONICS // GROUP // CHUNKS
-    rows = [groups * blocks * ROWS + (ROWS if c == 0 else 0) for c in range(CHUNKS)]
-    table = jnp.asarray(half_table(angles))
+    rows = groups * blocks * ROWS + PAD
+    table = jnp.asarray(np.stack([half_table(angles, 0), half_table(angles, HARMONICS // CHUNKS)]))
     return pl.pallas_call(
         spectra_kernel,
-        out_shape=[jax.ShapeDtypeStruct((r, LANES), jnp.bfloat16) for r in rows],
+        out_shape=[jax.ShapeDtypeStruct((rows, LANES), jnp.bfloat16)] * CHUNKS,
         in_specs=[
+            pl.BlockSpec(memory_space=pltpu.SMEM),
             pl.BlockSpec(memory_space=pltpu.SMEM),
             pl.BlockSpec(memory_space=pltpu.HBM),
             pl.BlockSpec(memory_space=pltpu.HBM),
@@ -102,7 +103,7 @@
         out_specs=[pl.BlockSpec(memory_space=pltpu.VMEM)] * CHUNKS,
         scratch_shapes=[
             pltpu.VMEM((shots * blocks, LANES, angles), jnp.float32),
-            pltpu.VMEM(table.shape, jnp.bfloat16),
+            pltpu.VMEM(table.shape[1:], jnp.bfloat16),
             pltpu.VMEM((2, shots, 2 * LANES, angles // 2), jnp.bfloat16),
             pltpu.SemaphoreType.DMA((shots * blocks + 1,)),
         ],
@@ -111,31 +112,34 @@
             flops=8 * shots * cycles * angles * LANES, bytes_accessed=frames.size * 4, transcendentals=0
         ),
         name="spectra",
-    )(valid_mask, frames, table)
-
-
-def correlate_kernel(tail, start_ref, *refs):
+    )(valid_mask, core, frames, table)
+
+
+def correlate_kernel(place_ref, *refs):
     out_ref, left, inverse = refs[-3:]
     n = left.shape[2] // ROWS
-    pieces, firsts = refs[:n], refs[n : 2 * n]
+    pairs = refs[: n // 2]
     per_step = out_ref.shape[0] // GROUP
     width, cycles = out_ref.shape[1:]
     blocks = cycles // LANES
     wide = GROUP * width
+    rows = pairs[0].shape[0] // 2
     step = pl.program_id(0)
 
     def tiles(group, q):
-        where = pl.ds(pl.multiple_of((group * blocks + q) * ROWS, ROWS), ROWS)
-        return jnp.concatenate([piece[where, :] for piece in pieces], axis=0)
+        at = (group * blocks + q) * ROWS
+        return jnp.concatenate(
+            [pair[pl.ds(pl.multiple_of(at + half, PAD), ROWS), :] for pair in pairs for half in (0, rows)], axis=0
+        )
 
     @pl.when(step == 0)
     def _():
-        total = jnp.zeros((ROWS // 2, LANES), jnp.float32)
-        for first in firsts:
-            tile = first[pl.ds(tail, ROWS), :].astype(jnp.float32)
-            total += tile[: ROWS // 2] + tile[ROWS // 2 :]
+        total = jnp.zeros((PAD, LANES), jnp.float32)
+        for pair in pairs:
+            for half in (rows, 2 * rows):
+                total += pair[pl.ds(half - PAD, PAD), :].astype(jnp.float32)
         inverse[...] = 1.0 / total
-        start = start_ref[0]
+        start = place_ref[0]
         lane = lax.broadcasted_iota(jnp.int32, (wide, LANES), 1)
         line = lax.broadcasted_iota(jnp.int32, (wide, LANES), 0)
         pick = jnp.where(lane == start % LANES + line % width, 1.0, 0.0).astype(jnp.bfloat16)
@@ -164,28 +168,31 @@
         out_ref[pl.ds(u * GROUP, GROUP)] = product.reshape(GROUP, width, cycles)
 
 
-def correlate_call(start, pieces, firsts, before, chunk, cycles, tail):
-    n = len(pieces)
+def correlate_call(place, pairs, before, cycles):
+    n = 2 * len(pairs)
     width = cycles // n
     groups = HARMONICS // GROUP // CHUNKS
     steps = groups // 2
-    operands = [start, *pieces, *firsts]
-    specs = [pl.BlockSpec(memory_space=pltpu.SMEM)] + [pl.BlockSpec(memory_space=pltpu.VMEM)] * (2 * n)
+    operands = [place, *pairs]
+    specs = [pl.BlockSpec(memory_space=pltpu.VMEM)] * len(pairs)
     aliases = {}
     if before is not None:
         aliases = {len(operands): 0}
         operands.append(before)
         specs.append(pl.BlockSpec(memory_space=pl.ANY))
     return pl.pallas_call(
-        functools.partial(correlate_kernel, tail),
+        correlate_kernel,
         out_shape=jax.ShapeDtypeStruct((HARMONICS, width, cycles), jnp.float32),
-        grid=(steps,),
-        in_specs=specs,
-        out_specs=pl.BlockSpec((2 * GROUP, width, cycles), lambda g: (g + chunk * steps, 0, 0)),
-        scratch_shapes=[
-            pltpu.VMEM((groups, 2 * GROUP * width, n * ROWS), jnp.bfloat16),
-            pltpu.VMEM((ROWS // 2, LANES), jnp.float32),
-        ],
+        grid_spec=pltpu.PrefetchScalarGridSpec(
+            num_scalar_prefetch=1,
+            grid=(steps,),
+            in_specs=specs,
+            out_specs=pl.BlockSpec((2 * GROUP, width, cycles), lambda g, at: (g + at[1] * steps, 0, 0)),
+            scratch_shapes=[
+                pltpu.VMEM((groups, 2 * GROUP * width, n * ROWS), jnp.bfloat16),
+                pltpu.VMEM((PAD, LANES), jnp.float32),
+            ],
+        ),
         input_output_aliases=aliases,
         compiler_params=pltpu.CompilerParams(vmem_limit_bytes=24 << 20),
         cost_estimate=pl.CostEstimate(
@@ -204,38 +211,41 @@
     return place
 
 
-def gather(piece, n, chunk):
+def move(x, pairs):
+    return lax.ppermute(x, "pb", pairs)
+
+
+def hops(n):
+    return n // 4
+
+
+def gather(mine, n):
     chips = n // 2
     place = {chip_at(p, chips): p for p in range(chips)}
-    ring = {
-        sign: [(i, 2 * chip_at(place[i // 2] + sign, chips) + i % 2) for i in range(n)] for sign in (1, -1)
-    }
+    ring = [(i, 2 * chip_at(place[i // 2] + (-1 if i % 2 else 1), chips) + i % 2) for i in range(n)]
     cores = [(i, i ^ 1) for i in range(n)]
-    held = [piece]
-    for sign in (1, -1):
-        moving = piece
-        hops = chips // 2 if (sign == 1) == (chunk % 2 == 0) else chips // 2 - 1
-        for _ in range(hops):
-            moving = lax.ppermute(moving, "pb", ring[sign])
-            held.append(moving)
-    return held + [lax.ppermute(x, "pb", cores) for x in held]
+    theirs = [move(mine[1], cores), move(mine[0], cores)]
+    first = [jnp.concatenate([mine[0], theirs[0]], axis=0)]
+    second = [jnp.concatenate([mine[1], theirs[1]], axis=0)]
+    for i in range(1, hops(n) + 1):
+        first.append(move(first[-1], ring))
+        if i < hops(n):
+            second.append(move(second[-1], ring))
+    crossed = [[move(x, cores) for x in held[1:]] for held in (first, second)]
+    return first + crossed[1], second + crossed[0]
 
 
 def body(frames, valid_mask):
-    shots, cycles, angles = frames.shape
+    _, cycles, _ = frames.shape
     n = lax.axis_size("pb")
-    parts = spectra_call(frames, valid_mask)
-    start = (lax.axis_index("pb") * (cycles // n)).astype(jnp.int32).reshape(1)
-    held = [gather(part, n, chunk) for chunk, part in enumerate(parts)]
-    tail = parts[0].shape[0] - ROWS
-    out = None
-    for chunk in range(CHUNKS):
-        out = correlate_call(start, held[chunk], held[0], out, chunk, cycles, tail)
-    return out
+    index = lax.axis_index("pb").astype(jnp.int32)
+    core = index % 2
+    first, second = gather(spectra_call(frames, valid_mask, core.reshape(1)), n)
+    start = index * (cycles // n)
+    out = correlate_call(jnp.stack([start, core]), first, None, cycles)
+    return correlate_call(jnp.stack([start, 1 - core]), second, out, cycles)
 
 
 def solution(mesh):
     placed = (P(("groups", "pb"), None, None), P(("groups", "pb")))
-    return jax.shard_map(
-        body, mesh=mesh, in_specs=placed, out_specs=P("groups", "pb", None), check_vma=False
-    )
+    return jax.shard_map(body, mesh=mesh, in_specs=placed, out_specs=P("groups", "pb", None), check_vma=False)

time: 51.7 us -> 43.4 us (0.84)
  waiting for transfers between devices: 15.1 us -> 9.75 us
  starting transfers between devices: 21.8 us -> 16.7 us
  Pallas kernels: 13.7 us -> 14.8 us
  local copies, waits for them, and re-layouts: 0.91 us -> 1.87 us
    ppermute x30 -> x16, waiting for transfers between devices: 15.1 us -> 9.75 us  [move(): return lax.ppermute(x, 'pb', pairs)]
    ppermute x30 -> x16, starting transfers between devices: 21.8 us -> 16.7 us  [move(): return lax.ppermute(x, 'pb', pairs)]
    pallas_call x3, Pallas kernels: 13.7 us -> 14.8 us  [the longest x2 8.79 us: correlate_call(): pl.pallas_call(correlate_kernel, out_shape=jax.ShapeDtypeStruct((HARMONIC...]
    unnamed x4 -> x2, local copies, waits for them, and re-layouts: 0.91 us -> 1.83 us
  transfers between devices with their start and end apart: 30 -> 16, of which waited for: 8 -> 8; matrix products, arithmetic and copies ran while one was open for 0% -> 4% of each run, Pallas kernels for 6% -> 9%
where the time goes in v3:
time: 43.4 us; the launch traced here: 43.2 us
  starting transfers between devices  16.7 us (38%)
  Pallas kernels  14.8 us (34%)
  waiting for transfers between devices  9.75 us (22%)
  local copies, waits for them, and re-layouts  1.87 us (4%)
    ppermute x16, starting transfers between devices, move(): return lax.ppermute(x, 'pb', pairs)  16.7 us
    ppermute x16, waiting for transfers between devices, move(): return lax.ppermute(x, 'pb', pairs)  9.75 us
    pallas_call x2, Pallas kernels, correlate_call(): pl.pallas_call(correlate_kernel, out_shape=jax.ShapeDtypeStruct((HARMONIC...  8.79 us
    pallas_call x1, Pallas kernels, spectra_call(): pl.pallas_call(spectra_kernel, out_shape=[jax.ShapeDtypeStruct((rows, LAN...  6 us
    unnamed x2, local copies, waits for them, and re-layouts  1.83 us
  transfers between devices with their start and end apart: 16, of which 8 were waited for; matrix products, arithmetic and copies ran while one was open for 4% of the time, Pallas kernels for 9%

profile of v3, /device:TPU:0, one launch (start us, length us, event | category | flops | bytes accessed | tf_op | source)
XLA Modules:
  0.0 43.2 jit_solution(2046649196493684329)
XLA Ops:
  0.0 6.0 %spectra.1 = (bf16[520,128]{1,0:T(8,128)(2,1)}, bf16[520,128]{1,0:T(8,128)(2,1)}) custom-call(s32[2]{0:T(128)} %mask_ref.1, s32[1]{0:T(128)} %bitcast.2.core_ref, f32[2,512,2048]{2,1,0:T(8,128)} %frames_ref.1, bf16[2,1024,256]{2,1,0:T(8,128)(2,1)} %constant.22.clone.table_ref), custom_call_target="tpu_custom_call" | custom-call | flops 2147483648 | bytes 8388608 | tf_op jit(solution)/shard_map/spectra/pallas_call | solution.py:94
  6.0 0.6 %collective-permute-start.4 = (bf16[520,128]{1,0:T(8,128)(2,1)}, bf16[520,128]{1,0:T(8,128)(2,1)S(1)}, u32[]{:S(2)}, u32[]{:S(2)}) collective-permute-start(bf16[520,128]{1,0:T(8,128)(2,1)} %get-tuple-element.7), channel_id=1, source_target_pairs={{0,1},{1,0},{2,3},{3,2},{4,5},{5,4},{6,7},{7,6},{8,9},{9,8},{10,11... | collective-permute-start | bytes 399368 | tf_op jit(solution)/shard_map/ppermute | solution.py:215
  6.6 0.1 collective-permute-start
  6.6 0.9 %constant_dynamic-update-slice_fusion.3 = bf16[1040,128]{1,0:T(8,128)(2,1)S(1)} fusion(bf16[520,128]{1,0:T(8,128)(2,1)} %get-tuple-element.8), kind=kLoop, calls=%fused_computation.3 | loop fusion | bytes 266240
  7.6 0.2 collective-permute-done.4
  7.8 3.0 %collective-permute-start.5 = (bf16[1040,128]{1,0:T(8,128)(2,1)S(1)}, bf16[1040,128]{1,0:T(8,128)(2,1)S(1)}, u32[]{:S(2)}, u32[]{:S(2)}) collective-permute-start(bf16[1040,128]{1,0:T(8,128)(2,1)S(1)} %constant_dynamic-update-slice_fusion.2.refs_0_), channel_id=1, source_target_pairs={{0,4},{1,3},{2,0},{3,7},{4,8},{5,1},{6,2},{7,11},{8,12},{9,5},{10,... | collective-permute-start | bytes 798728 | tf_op jit(solution)/shard_map/ppermute | solution.py:215
  10.8 0.9 %constant_dynamic-update-slice_fusion.1 = bf16[1040,128]{1,0:T(8,128)(2,1)S(1)} fusion(bf16[520,128]{1,0:T(8,128)(2,1)} %get-tuple-element.7), kind=kLoop, calls=%fused_computation.1 | loop fusion | bytes 266240
  11.7 0.0 collective-permute-done
  11.7 1.6 %collective-permute-start.1 = (bf16[1040,128]{1,0:T(8,128)(2,1)S(1)}, bf16[1040,128]{1,0:T(8,128)(2,1)S(1)}, u32[]{:S(2)}, u32[]{:S(2)}) collective-permute-start(bf16[1040,128]{1,0:T(8,128)(2,1)S(1)} %constant_dynamic-update-slice_fusion.refs_0_), channel_id=1, source_target_pairs={{0,4},{1,3},{2,0},{3,7},{4,8},{5,1},{6,2},{7,11},{8,12},{9,5},{10,... | collective-permute-start | bytes 798728 | tf_op jit(solution)/shard_map/ppermute | solution.py:215
  13.3 1.7 %collective-permute-done.5.refs_1_ = bf16[1040,128]{1,0:T(8,128)(2,1)S(1)} collective-permute-done((bf16[1040,128]{1,0:T(8,128)(2,1)S(1)}, bf16[1040,128]{1,0:T(8,128)(2,1)S(1)}, u32[]{:S(2)}, u32[]{:S(2)}) %collective-permute-start.5) | collective-permute-done | bytes 266272 | tf_op jit(solution)/shard_map/ppermute | solution.py:215
  15.1 2.1 %collective-permute-start.7 = (bf16[1040,128]{1,0:T(8,128)(2,1)S(1)}, bf16[1040,128]{1,0:T(8,128)(2,1)S(1)}, u32[]{:S(2)}, u32[]{:S(2)}) collective-permute-start(bf16[1040,128]{1,0:T(8,128)(2,1)S(1)} %collective-permute-done.5.refs_1_), channel_id=1, source_target_pairs={{0,4},{1,3},{2,0},{3,7},{4,8},{5,1},{6,2},{7,11},{8,12},{9,5},{10,... | collective-permute-start | bytes 798728 | tf_op jit(solution)/shard_map/ppermute | solution.py:215
  17.2 1.0 %collective-permute-done.1.refs_1_ = bf16[1040,128]{1,0:T(8,128)(2,1)S(1)} collective-permute-done((bf16[1040,128]{1,0:T(8,128)(2,1)S(1)}, bf16[1040,128]{1,0:T(8,128)(2,1)S(1)}, u32[]{:S(2)}, u32[]{:S(2)}) %collective-permute-start.1) | collective-permute-done | bytes 266272 | tf_op jit(solution)/shard_map/ppermute | solution.py:215
  18.2 1.8 %collective-permute-start.2 = (bf16[1040,128]{1,0:T(8,128)(2,1)S(1)}, bf16[1040,128]{1,0:T(8,128)(2,1)S(1)}, u32[]{:S(2)}, u32[]{:S(2)}) collective-permute-start(bf16[1040,128]{1,0:T(8,128)(2,1)S(1)} %collective-permute-done.1.refs_1_), channel_id=1, source_target_pairs={{0,4},{1,3},{2,0},{3,7},{4,8},{5,1},{6,2},{7,11},{8,12},{9,5},{10,... | collective-permute-start | bytes 798728 | tf_op jit(solution)/shard_map/ppermute | solution.py:215
  20.0 1.5 %collective-permute-done.7.refs_2_ = bf16[1040,128]{1,0:T(8,128)(2,1)S(1)} collective-permute-done((bf16[1040,128]{1,0:T(8,128)(2,1)S(1)}, bf16[1040,128]{1,0:T(8,128)(2,1)S(1)}, u32[]{:S(2)}, u32[]{:S(2)}) %collective-permute-start.7) | collective-permute-done | bytes 266272 | tf_op jit(solution)/shard_map/ppermute | solution.py:215
  21.5 2.1 %collective-permute-start.9 = (bf16[1040,128]{1,0:T(8,128)(2,1)S(1)}, bf16[1040,128]{1,0:T(8,128)(2,1)S(1)}, u32[]{:S(2)}, u32[]{:S(2)}) collective-permute-start(bf16[1040,128]{1,0:T(8,128)(2,1)S(1)} %collective-permute-done.7.refs_2_), channel_id=1, source_target_pairs={{0,4},{1,3},{2,0},{3,7},{4,8},{5,1},{6,2},{7,11},{8,12},{9,5},{10,... | collective-permute-start | bytes 798728 | tf_op jit(solution)/shard_map/ppermute | solution.py:215
  23.6 1.0 %collective-permute-done.2.refs_2_ = bf16[1040,128]{1,0:T(8,128)(2,1)S(1)} collective-permute-done((bf16[1040,128]{1,0:T(8,128)(2,1)S(1)}, bf16[1040,128]{1,0:T(8,128)(2,1)S(1)}, u32[]{:S(2)}, u32[]{:S(2)}) %collective-permute-start.2) | collective-permute-done | bytes 266272 | tf_op jit(solution)/shard_map/ppermute | solution.py:215
  24.6 1.8 %collective-permute-start.3 = (bf16[1040,128]{1,0:T(8,128)(2,1)S(1)}, bf16[1040,128]{1,0:T(8,128)(2,1)S(1)}, u32[]{:S(2)}, u32[]{:S(2)}) collective-permute-start(bf16[1040,128]{1,0:T(8,128)(2,1)S(1)} %collective-permute-done.2.refs_2_), channel_id=1, source_target_pairs={{0,4},{1,3},{2,0},{3,7},{4,8},{5,1},{6,2},{7,11},{8,12},{9,5},{10,... | collective-permute-start | bytes 798728 | tf_op jit(solution)/shard_map/ppermute | solution.py:215
  26.4 0.0 collective-permute-start.13
  26.4 0.5 %collective-permute-start.14 = (bf16[1040,128]{1,0:T(8,128)(2,1)S(1)}, bf16[1040,128]{1,0:T(8,128)(2,1)S(1)}, u32[]{:S(2)}, u32[]{:S(2)}) collective-permute-start(bf16[1040,128]{1,0:T(8,128)(2,1)S(1)} %collective-permute-done.2.refs_2_), channel_id=1, source_target_pairs={{0,1},{1,0},{2,3},{3,2},{4,5},{5,4},{6,7},{7,6},{8,9},{9,8},{10,11... | collective-permute-start | bytes 798728 | tf_op jit(solution)/shard_map/ppermute | solution.py:215
  27.0 1.0 %collective-permute-done.9.refs_3_ = bf16[1040,128]{1,0:T(8,128)(2,1)S(1)} collective-permute-done((bf16[1040,128]{1,0:T(8,128)(2,1)S(1)}, bf16[1040,128]{1,0:T(8,128)(2,1)S(1)}, u32[]{:S(2)}, u32[]{:S(2)}) %collective-permute-start.9) | collective-permute-done | bytes 266272 | tf_op jit(solution)/shard_map/ppermute | solution.py:215
  27.9 2.1 %collective-permute-start.11 = (bf16[1040,128]{1,0:T(8,128)(2,1)S(1)}, bf16[1040,128]{1,0:T(8,128)(2,1)S(1)}, u32[]{:S(2)}, u32[]{:S(2)}) collective-permute-start(bf16[1040,128]{1,0:T(8,128)(2,1)S(1)} %collective-permute-done.9.refs_3_), channel_id=1, source_target_pairs={{0,4},{1,3},{2,0},{3,7},{4,8},{5,1},{6,2},{7,11},{8,12},{9,5},{10,... | collective-permute-start | bytes 798728 | tf_op jit(solution)/shard_map/ppermute | solution.py:215
  30.0 1.0 %collective-permute-done.3.refs_3_ = bf16[1040,128]{1,0:T(8,128)(2,1)S(1)} collective-permute-done((bf16[1040,128]{1,0:T(8,128)(2,1)S(1)}, bf16[1040,128]{1,0:T(8,128)(2,1)S(1)}, u32[]{:S(2)}, u32[]{:S(2)}) %collective-permute-start.3) | collective-permute-done | bytes 266272 | tf_op jit(solution)/shard_map/ppermute | solution.py:215
  31.0 0.0 collective-permute-start.15
  31.0 0.5 %collective-permute-start.6 = (bf16[1040,128]{1,0:T(8,128)(2,1)S(1)}, bf16[1040,128]{1,0:T(8,128)(2,1)S(1)}, u32[]{:S(2)}, u32[]{:S(2)}) collective-permute-start(bf16[1040,128]{1,0:T(8,128)(2,1)S(1)} %collective-permute-done.5.refs_1_), channel_id=1, source_target_pairs={{0,1},{1,0},{2,3},{3,2},{4,5},{5,4},{6,7},{7,6},{8,9},{9,8},{10,11... | collective-permute-start | bytes 798728 | tf_op jit(solution)/shard_map/ppermute | solution.py:215
  31.5 0.0 collective-permute-done.13.refs_5_
  31.5 0.0 collective-permute-start.8
  31.5 0.0 collective-permute-done.14.refs_6_
  31.5 0.5 %collective-permute-start.10 = (bf16[1040,128]{1,0:T(8,128)(2,1)S(1)}, bf16[1040,128]{1,0:T(8,128)(2,1)}, u32[]{:S(2)}, u32[]{:S(2)}) collective-permute-start(bf16[1040,128]{1,0:T(8,128)(2,1)S(1)} %collective-permute-done.9.refs_3_), channel_id=1, source_target_pairs={{0,1},{1,0},{2,3},{3,2},{4,5},{5,4},{6,7},{7,6},{8,9},{9,8},{10,11... | collective-permute-start | bytes 798728 | tf_op jit(solution)/shard_map/ppermute | solution.py:215
  32.0 2.3 %collective-permute-done.11.refs_4_ = bf16[1040,128]{1,0:T(8,128)(2,1)S(1)} collective-permute-done((bf16[1040,128]{1,0:T(8,128)(2,1)S(1)}, bf16[1040,128]{1,0:T(8,128)(2,1)S(1)}, u32[]{:S(2)}, u32[]{:S(2)}) %collective-permute-start.11) | collective-permute-done | bytes 266272 | tf_op jit(solution)/shard_map/ppermute | solution.py:215
  34.3 0.0 collective-permute-start.12
  34.3 0.1 pad_add_fusion
  34.4 0.0 collective-permute-done.15.refs_7_
  34.4 3.8 %correlate.2.refs_8_ = f32[64,32,512]{2,1,0:T(8,128)} custom-call(s32[2]{0:T(128)S(1)} %get-tuple-element.10.place_ref, bf16[1040,128]{1,0:T(8,128)(2,1)S(1)} %constant_dynamic-update-slice_fusion.2.refs_0_, bf16[1040,128]{1,0:T(8,128)(2,1)S(1)} %collective-permute-done.5.refs_1_, bf16[1040,128]{1,0:T(8,128)(2,1)S(1)} %collective-permute-done.7.refs_2_, ...), custom_call_target="tpu_custom_call" | custom-call | flops 268435456 | bytes 2097152 | tf_op jit(solution)/shard_map/correlate/pallas_call | solution.py:183
  38.3 0.0 collective-permute-done.6.refs_4_
  38.3 0.0 collective-permute-done.8.refs_5_
  38.3 0.0 collective-permute-done.10.refs_6_
  38.3 0.0 collective-permute-done.12.refs_7_
  38.3 5.0 %correlate.3 = f32[64,32,512]{2,1,0:T(8,128)} custom-call(s32[2]{0:T(128)S(1)} %get-tuple-element.9.place_ref, bf16[1040,128]{1,0:T(8,128)(2,1)S(1)} %constant_dynamic-update-slice_fusion.refs_0_, bf16[1040,128]{1,0:T(8,128)(2,1)S(1)} %collective-permute-done.1.refs_1_, ...), custom_call_target="tpu_custom_call", output_to_operand_aliasing={{}: (9, {})} | custom-call | flops 268435456 | bytes 2097152 | tf_op jit(solution)/shard_map/correlate/pallas_call | solution.py:183
  (2 shorter events, 0.0 us)
Async XLA Ops:
  6.0 1.8 %collective-permute-start.4 = (bf16[520,128]{1,0:T(8,128)(2,1)}, bf16[520,128]{1,0:T(8,128)(2,1)S(1)}, u32[]{:S(2)}, u32[]{:S(2)}) collective-permute-start(bf16[520,128]{1,0:T(8,128)(2,1)} %get-tuple-element.7), channel_id=1, source_target_pairs={{0,1},{1,0},{2,3},{3,2},{4,5},{5,4},{6,7},{7,6},{8,9},{9,8},{10,11... | collective-permute-start | bytes 399368 | tf_op jit(solution)/shard_map/ppermute | solution.py:215
  6.6 5.1 %collective-permute-start = (bf16[520,128]{1,0:T(8,128)(2,1)}, bf16[520,128]{1,0:T(8,128)(2,1)S(1)}, u32[]{:S(2)}, u32[]{:S(2)}) collective-permute-start(bf16[520,128]{1,0:T(8,128)(2,1)} %get-tuple-element.8), channel_id=1, source_target_pairs={{0,1},{1,0},{2,3},{3,2},{4,5},{5,4},{6,7},{7,6},{8,9},{9,8},{10,11... | collective-permute-start | bytes 399368 | tf_op jit(solution)/shard_map/ppermute | solution.py:215
  7.8 7.3 %collective-permute-start.5 = (bf16[1040,128]{1,0:T(8,128)(2,1)S(1)}, bf16[1040,128]{1,0:T(8,128)(2,1)S(1)}, u32[]{:S(2)}, u32[]{:S(2)}) collective-permute-start(bf16[1040,128]{1,0:T(8,128)(2,1)S(1)} %constant_dynamic-update-slice_fusion.2.refs_0_), channel_id=1, source_target_pairs={{0,4},{1,3},{2,0},{3,7},{4,8},{5,1},{6,2},{7,11},{8,12},{9,5},{10,... | collective-permute-start | bytes 798728 | tf_op jit(solution)/shard_map/ppermute | solution.py:215
  11.7 6.5 %collective-permute-start.1 = (bf16[1040,128]{1,0:T(8,128)(2,1)S(1)}, bf16[1040,128]{1,0:T(8,128)(2,1)S(1)}, u32[]{:S(2)}, u32[]{:S(2)}) collective-permute-start(bf16[1040,128]{1,0:T(8,128)(2,1)S(1)} %constant_dynamic-update-slice_fusion.refs_0_), channel_id=1, source_target_pairs={{0,4},{1,3},{2,0},{3,7},{4,8},{5,1},{6,2},{7,11},{8,12},{9,5},{10,... | collective-permute-start | bytes 798728 | tf_op jit(solution)/shard_map/ppermute | solution.py:215
  15.1 6.4 %collective-permute-start.7 = (bf16[1040,128]{1,0:T(8,128)(2,1)S(1)}, bf16[1040,128]{1,0:T(8,128)(2,1)S(1)}, u32[]{:S(2)}, u32[]{:S(2)}) collective-permute-start(bf16[1040,128]{1,0:T(8,128)(2,1)S(1)} %collective-permute-done.5.refs_1_), channel_id=1, source_target_pairs={{0,4},{1,3},{2,0},{3,7},{4,8},{5,1},{6,2},{7,11},{8,12},{9,5},{10,... | collective-permute-start | bytes 798728 | tf_op jit(solution)/shard_map/ppermute | solution.py:215
  18.2 6.4 %collective-permute-start.2 = (bf16[1040,128]{1,0:T(8,128)(2,1)S(1)}, bf16[1040,128]{1,0:T(8,128)(2,1)S(1)}, u32[]{:S(2)}, u32[]{:S(2)}) collective-permute-start(bf16[1040,128]{1,0:T(8,128)(2,1)S(1)} %collective-permute-done.1.refs_1_), channel_id=1, source_target_pairs={{0,4},{1,3},{2,0},{3,7},{4,8},{5,1},{6,2},{7,11},{8,12},{9,5},{10,... | collective-permute-start | bytes 798728 | tf_op jit(solution)/shard_map/ppermute | solution.py:215
  21.5 6.4 %collective-permute-start.9 = (bf16[1040,128]{1,0:T(8,128)(2,1)S(1)}, bf16[1040,128]{1,0:T(8,128)(2,1)S(1)}, u32[]{:S(2)}, u32[]{:S(2)}) collective-permute-start(bf16[1040,128]{1,0:T(8,128)(2,1)S(1)} %collective-permute-done.7.refs_2_), channel_id=1, source_target_pairs={{0,4},{1,3},{2,0},{3,7},{4,8},{5,1},{6,2},{7,11},{8,12},{9,5},{10,... | collective-permute-start | bytes 798728 | tf_op jit(solution)/shard_map/ppermute | solution.py:215
  24.6 6.4 %collective-permute-start.3 = (bf16[1040,128]{1,0:T(8,128)(2,1)S(1)}, bf16[1040,128]{1,0:T(8,128)(2,1)S(1)}, u32[]{:S(2)}, u32[]{:S(2)}) collective-permute-start(bf16[1040,128]{1,0:T(8,128)(2,1)S(1)} %collective-permute-done.2.refs_2_), channel_id=1, source_target_pairs={{0,4},{1,3},{2,0},{3,7},{4,8},{5,1},{6,2},{7,11},{8,12},{9,5},{10,... | collective-permute-start | bytes 798728 | tf_op jit(solution)/shard_map/ppermute | solution.py:215
  26.4 5.1 %collective-permute-start.13 = (bf16[1040,128]{1,0:T(8,128)(2,1)S(1)}, bf16[1040,128]{1,0:T(8,128)(2,1)S(1)}, u32[]{:S(2)}, u32[]{:S(2)}) collective-permute-start(bf16[1040,128]{1,0:T(8,128)(2,1)S(1)} %collective-permute-done.1.refs_1_), channel_id=1, source_target_pairs={{0,1},{1,0},{2,3},{3,2},{4,5},{5,4},{6,7},{7,6},{8,9},{9,8},{10,11... | collective-permute-start | bytes 798728 | tf_op jit(solution)/shard_map/ppermute | solution.py:215
  26.4 5.1 %collective-permute-start.14 = (bf16[1040,128]{1,0:T(8,128)(2,1)S(1)}, bf16[1040,128]{1,0:T(8,128)(2,1)S(1)}, u32[]{:S(2)}, u32[]{:S(2)}) collective-permute-start(bf16[1040,128]{1,0:T(8,128)(2,1)S(1)} %collective-permute-done.2.refs_2_), channel_id=1, source_target_pairs={{0,1},{1,0},{2,3},{3,2},{4,5},{5,4},{6,7},{7,6},{8,9},{9,8},{10,11... | collective-permute-start | bytes 798728 | tf_op jit(solution)/shard_map/ppermute | solution.py:215
  27.9 6.4 %collective-permute-start.11 = (bf16[1040,128]{1,0:T(8,128)(2,1)S(1)}, bf16[1040,128]{1,0:T(8,128)(2,1)S(1)}, u32[]{:S(2)}, u32[]{:S(2)}) collective-permute-start(bf16[1040,128]{1,0:T(8,128)(2,1)S(1)} %collective-permute-done.9.refs_3_), channel_id=1, source_target_pairs={{0,4},{1,3},{2,0},{3,7},{4,8},{5,1},{6,2},{7,11},{8,12},{9,5},{10,... | collective-permute-start | bytes 798728 | tf_op jit(solution)/shard_map/ppermute | solution.py:215
  31.0 3.4 %collective-permute-start.15 = (bf16[1040,128]{1,0:T(8,128)(2,1)S(1)}, bf16[1040,128]{1,0:T(8,128)(2,1)S(1)}, u32[]{:S(2)}, u32[]{:S(2)}) collective-permute-start(bf16[1040,128]{1,0:T(8,128)(2,1)S(1)} %collective-permute-done.3.refs_3_), channel_id=1, source_target_pairs={{0,1},{1,0},{2,3},{3,2},{4,5},{5,4},{6,7},{7,6},{8,9},{9,8},{10,11... | collective-permute-start | bytes 798728 | tf_op jit(solution)/shard_map/ppermute | solution.py:215
  31.0 7.2 %collective-permute-start.6 = (bf16[1040,128]{1,0:T(8,128)(2,1)S(1)}, bf16[1040,128]{1,0:T(8,128)(2,1)S(1)}, u32[]{:S(2)}, u32[]{:S(2)}) collective-permute-start(bf16[1040,128]{1,0:T(8,128)(2,1)S(1)} %collective-permute-done.5.refs_1_), channel_id=1, source_target_pairs={{0,1},{1,0},{2,3},{3,2},{4,5},{5,4},{6,7},{7,6},{8,9},{9,8},{10,11... | collective-permute-start | bytes 798728 | tf_op jit(solution)/shard_map/ppermute | solution.py:215
  31.5 6.7 %collective-permute-start.8 = (bf16[1040,128]{1,0:T(8,128)(2,1)S(1)}, bf16[1040,128]{1,0:T(8,128)(2,1)}, u32[]{:S(2)}, u32[]{:S(2)}) collective-permute-start(bf16[1040,128]{1,0:T(8,128)(2,1)S(1)} %collective-permute-done.7.refs_2_), channel_id=1, source_target_pairs={{0,1},{1,0},{2,3},{3,2},{4,5},{5,4},{6,7},{7,6},{8,9},{9,8},{10,11... | collective-permute-start | bytes 798728 | tf_op jit(solution)/shard_map/ppermute | solution.py:215
  31.5 6.7 %collective-permute-start.10 = (bf16[1040,128]{1,0:T(8,128)(2,1)S(1)}, bf16[1040,128]{1,0:T(8,128)(2,1)}, u32[]{:S(2)}, u32[]{:S(2)}) collective-permute-start(bf16[1040,128]{1,0:T(8,128)(2,1)S(1)} %collective-permute-done.9.refs_3_), channel_id=1, source_target_pairs={{0,1},{1,0},{2,3},{3,2},{4,5},{5,4},{6,7},{7,6},{8,9},{9,8},{10,11... | collective-permute-start | bytes 798728 | tf_op jit(solution)/shard_map/ppermute | solution.py:215
  34.3 3.9 %collective-permute-start.12 = (bf16[1040,128]{1,0:T(8,128)(2,1)S(1)}, bf16[1040,128]{1,0:T(8,128)(2,1)}, u32[]{:S(2)}, u32[]{:S(2)}) collective-permute-start(bf16[1040,128]{1,0:T(8,128)(2,1)S(1)} %collective-permute-done.11.refs_4_), channel_id=1, source_target_pairs={{0,1},{1,0},{2,3},{3,2},{4,5},{5,4},{6,7},{7,6},{8,9},{9,8},{10,11... | collective-permute-start | bytes 798728 | tf_op jit(solution)/shard_map/ppermute | solution.py:215

commit v4 on v3

v4 whole, which is shorter than its diff:
```python
import functools
import math

import jax
import jax.numpy as jnp
import numpy as np
from jax import lax
from jax.experimental import pallas as pl
from jax.experimental.pallas import tpu as pltpu
from jax.sharding import PartitionSpec as P

HARMONICS = 64
LANES = 128
GROUP = 4
ROWS = 4 * GROUP
CHUNKS = 2
PAD = 8
DEPTH = 256


def half_table(angles, first):
    order = 2 * ((np.arange(HARMONICS) + first) % HARMONICS + 1)
    wrapped = np.arange(angles // 2)[:, None] * order[None, :] % angles
    phase = wrapped * (2.0 * math.pi / angles)
    table = np.stack([np.cos(phase), -np.sin(phase)], axis=-1).reshape(angles // 2, 2 * HARMONICS)
    table = (2.0 / math.sqrt(angles)) * table
    high = table.astype(jnp.bfloat16)
    low = (table - high.astype(np.float64)).astype(jnp.bfloat16)
    return np.concatenate([high, low], axis=1)


def spectra_kernel(mask_ref, frames_ref, table_ref, *refs):
    out_refs = refs[:CHUNKS]
    buf, table, halves, mask, sems = refs[CHUNKS:]
    shots, cycles, angles = frames_ref.shape
    blocks = cycles // LANES
    half = angles // 2
    groups = HARMONICS // GROUP // CHUNKS
    tick = pltpu.make_async_copy(mask_ref, mask, sems.at[shots * blocks + 1])
    tick.start()
    core = lax.rem(lax.axis_index("pb"), 2)
    copies = [pltpu.make_async_copy(table_ref.at[core], table, sems.at[shots * blocks])]
    for q in range(blocks):
        for s in range(shots):
            copies.append(
                pltpu.make_async_copy(
                    frames_ref.at[s, pl.ds(q * LANES, LANES), :], buf.at[q * shots + s], sems.at[q * shots + s]
                )
            )
    for copy in copies:
        copy.start()
    tick.wait()
    weights = [mask[s].astype(jnp.float32) for s in range(shots)]
    count = jnp.full((PAD, LANES), weights[0] + weights[1], jnp.float32).astype(jnp.bfloat16)
    for out_ref in out_refs:
        out_ref[pl.ds(groups * blocks * ROWS, PAD), :] = count
    copies[0].wait()

    def split(q, s, k):
        scale = 0.5 * weights[s]
        x = buf.at[q * shots + s]
        folded = x[:, pl.ds(k, DEPTH)] * scale + x[:, pl.ds(half + k, DEPTH)] * scale
        high = folded.astype(jnp.bfloat16)
        halves[q % 2, s, pl.ds(0, LANES), pl.ds(k, DEPTH)] = high
        halves[q % 2, s, pl.ds(LANES, LANES), pl.ds(k, DEPTH)] = (folded - high.astype(jnp.float32)).astype(jnp.bfloat16)

    for s in range(shots):
        copies[1 + s].wait()
        for k in range(0, half, DEPTH):
            split(0, s, k)
    for q in range(blocks):
        if q + 1 < blocks:
            for s in range(shots):
                copies[1 + (q + 1) * shots + s].wait()
        pairs = [jnp.zeros((2 * LANES, 2 * LANES), jnp.float32)] * shots
        for k in range(0, half, DEPTH):
            for s in range(shots):
                pairs[s] += jnp.dot(
                    halves[q % 2, s, :, pl.ds(k, DEPTH)], table[pl.ds(k, DEPTH), :], preferred_element_type=jnp.float32
                )
                if q + 1 < blocks:
                    split(q + 1, s, k)
        turned = []
        for pair in pairs:
            pair = pair[:LANES] + pair[LANES:]
            turned.append((pair[:, :LANES] + pair[:, LANES:]).T)
        for g in range(HARMONICS // GROUP):
            part = slice(g * 2 * GROUP, (g + 1) * 2 * GROUP)
            block = jnp.concatenate([turned[0][part], turned[1][part]], axis=0).astype(jnp.bfloat16)
            out_refs[g // groups][pl.ds((g % groups * blocks + q) * ROWS, ROWS), :] = block


def spectra_call(frames, valid_mask):
    shots, cycles, angles = frames.shape
    blocks = cycles // LANES
    groups = HARMONICS // GROUP // CHUNKS
    rows = groups * blocks * ROWS + PAD
    table = jnp.asarray(np.stack([half_table(angles, 0), half_table(angles, HARMONICS // CHUNKS)]))
    return pl.pallas_call(
        spectra_kernel,
        out_shape=[jax.ShapeDtypeStruct((rows, LANES), jnp.bfloat16)] * CHUNKS,
        in_specs=[
            pl.BlockSpec(memory_space=pltpu.HBM),
            pl.BlockSpec(memory_space=pltpu.HBM),
            pl.BlockSpec(memory_space=pltpu.HBM),
        ],
        out_specs=[pl.BlockSpec(memory_space=pltpu.VMEM)] * CHUNKS,
        scratch_shapes=[
            pltpu.VMEM((shots * blocks, LANES, angles), jnp.float32),
            pltpu.VMEM(table.shape[1:], jnp.bfloat16),
            pltpu.VMEM((2, shots, 2 * LANES, angles // 2), jnp.bfloat16),
            pltpu.SMEM((shots,), jnp.int32),
            pltpu.SemaphoreType.DMA((shots * blocks + 2,)),
        ],
        compiler_params=pltpu.CompilerParams(vmem_limit_bytes=60 << 20),
        cost_estimate=pl.CostEstimate(
            flops=8 * shots * cycles * angles * LANES, bytes_accessed=frames.size * 4, transcendentals=0
        ),
        name="spectra",
    )(valid_mask, frames, table)


def correlate_kernel(turn, *refs):
    out_ref, left, results, sems = refs[-4:]
    groups, _, n = left.shape
    n //= ROWS
    pairs = refs[: n // 2]
    width, cycles = out_ref.shape[1:]
    blocks = cycles // LANES
    wide = GROUP * width
    rows = pairs[0].shape[0] // 2
    index = lax.axis_index("pb")
    start = index * width
    base = lax.rem(index + turn, 2) * (groups * GROUP)

    def tiles(group, q):
        at = (group * blocks + q) * ROWS
        at = at if isinstance(at, int) else pl.multiple_of(at, PAD)
        return jnp.concatenate([pair[pl.ds(at + half, ROWS), :] for pair in pairs for half in (0, rows)], axis=0)

    total = jnp.zeros((PAD, LANES), jnp.float32)
    for pair in pairs:
        for half in (rows, 2 * rows):
            total += pair[pl.ds(half - PAD, PAD), :].astype(jnp.float32)
    inverse = (1.0 / total)[:1, :]
    lane = lax.broadcasted_iota(jnp.int32, (wide, LANES), 1)
    line = lax.broadcasted_iota(jnp.int32, (wide, LANES), 0)
    pick = jnp.where(lane == lax.rem(start, LANES) + line % width, 1.0, 0.0).astype(jnp.bfloat16)
    lane = lax.broadcasted_iota(jnp.int32, (n * ROWS, LANES), 1)
    line = lax.broadcasted_iota(jnp.int32, (n * ROWS, LANES), 0)
    alike = jnp.where(lane % (2 * GROUP) == line % (2 * GROUP), 1.0, 0.0).astype(jnp.bfloat16)
    lane = lax.broadcasted_iota(jnp.int32, (wide, LANES), 1)
    line = lax.broadcasted_iota(jnp.int32, (wide, LANES), 0)
    kept = line // width == lane % (2 * GROUP) // 2
    kept = jnp.concatenate([kept] * (n * ROWS // LANES), axis=1)

    def prepare(g):
        own = tiles(g, lax.div(start, LANES))
        raw = lax.dot_general(pick, own, (((1,), (1,)), ((), ())), preferred_element_type=jnp.float32)
        sums = jnp.dot(raw.astype(jnp.bfloat16), alike, preferred_element_type=jnp.float32)
        mean = sums * inverse
        centred = raw - jnp.concatenate([mean] * (n * ROWS // LANES), axis=1)
        centred = jnp.where(kept, centred, 0.0)
        high = centred.astype(jnp.bfloat16)
        left[g, pl.ds(0, wide), :] = high
        left[g, pl.ds(wide, wide), :] = (centred - high.astype(jnp.float32)).astype(jnp.bfloat16)

    def copy(g):
        return pltpu.make_async_copy(results.at[g], out_ref.at[pl.ds(base + g * GROUP, GROUP)], sems.at[g])

    prepare(0)
    for g in range(groups):
        if g + 1 < groups:
            prepare(g + 1)
        for q in range(0, blocks, 2):
            right = jnp.concatenate([tiles(g, q), tiles(g, q + 1)], axis=1)
            both = jnp.dot(left[g], right, preferred_element_type=jnp.float32)
            product = (both[:wide] + both[wide:]) * inverse[:, :1]
            results[g, :, :, pl.ds(q * LANES, 2 * LANES)] = product.reshape(GROUP, width, 2 * LANES)
        copy(g).start()
    for g in range(groups):
        copy(g).wait()


def correlate_call(turn, pairs, before, cycles):
    n = 2 * len(pairs)
    width = cycles // n
    groups = HARMONICS // GROUP // CHUNKS
    operands = [*pairs]
    specs = [pl.BlockSpec(memory_space=pltpu.VMEM)] * len(pairs)
    aliases = {}
    if before is not None:
        aliases = {len(operands): 0}
        operands.append(before)
        specs.append(pl.BlockSpec(memory_space=pltpu.HBM))
    return pl.pallas_call(
        functools.partial(correlate_kernel, turn),
        out_shape=jax.ShapeDtypeStruct((HARMONICS, width, cycles), jnp.float32),
        in_specs=specs,
        out_specs=pl.BlockSpec(memory_space=pltpu.HBM),
        scratch_shapes=[
            pltpu.VMEM((groups, 2 * GROUP * width, n * ROWS), jnp.bfloat16),
            pltpu.VMEM((groups, GROUP, width, cycles), jnp.float32),
            pltpu.SemaphoreType.DMA((groups,)),
        ],
        input_output_aliases=aliases,
        compiler_params=pltpu.CompilerParams(vmem_limit_bytes=24 << 20),
        cost_estimate=pl.CostEstimate(
            flops=2 * HARMONICS // CHUNKS * width * cycles * n * ROWS,
            bytes_accessed=HARMONICS // CHUNKS * width * cycles * 4,
            transcendentals=0,
        ),
        name="correlate",
    )(*operands)


def chip_at(place, chips):
    place %= chips
    if chips == 8:
        return 2 * place if place < 4 else 2 * (7 - place) + 1
    return place


def move(x, pairs):
    return lax.ppermute(x, "pb", pairs)


def hops(n):
    return n // 4


def gather(mine, n):
    chips = n // 2
    place = {chip_at(p, chips): p for p in range(chips)}
    ring = [(i, 2 * chip_at(place[i // 2] + (-1 if i % 2 else 1), chips) + i % 2) for i in range(n)]
    cores = [(i, i ^ 1) for i in range(n)]
    theirs = [move(mine[1], cores), move(mine[0], cores)]
    first = [jnp.concatenate([mine[0], theirs[0]], axis=0)]
    second = [jnp.concatenate([mine[1], theirs[1]], axis=0)]
    for i in range(1, hops(n) + 1):
        first.append(move(first[-1], ring))
        if i < hops(n):
            second.append(move(second[-1], ring))
    crossed = [[move(x, cores) for x in held[1:]] for held in (first, second)]
    return first + crossed[1], second + crossed[0]


def body(frames, valid_mask):
    cycles = frames.shape[1]
    first, second = gather(spectra_call(frames, valid_mask), lax.axis_size("pb"))
    out = correlate_call(0, first, None, cycles)
    return correlate_call(1, second, out, cycles)


def solution(mesh):
    placed = (P(("groups", "pb"), None, None), P(("groups", "pb")))
    return jax.shard_map(body, mesh=mesh, in_specs=placed, out_specs=P("groups", "pb", None), check_vma=False)
```

time: 43.4 us -> 38.7 us (0.89)
  Pallas kernels: 14.8 us -> 10.1 us
    pallas_call x2, Pallas kernels: 8.79 us -> 4.78 us  [correlate_call(): pl.pallas_call(functools.partial(correlate_kernel, turn), out_shape=jax.S...]
    pallas_call x1, Pallas kernels: 6 us -> 5.35 us  [spectra_call(): pl.pallas_call(spectra_kernel, out_shape=[jax.ShapeDtypeStruct((rows, LAN...]
  transfers between devices with their start and end apart: 16 -> 16, of which waited for: 8 -> 8; matrix products, arithmetic and copies ran while one was open for 4% -> 5% of each run, Pallas kernels for 9% -> 6%
where the time goes in v4:
time: 38.7 us; the launch traced here: 38.5 us
  starting transfers between devices  16.7 us (43%)
  Pallas kernels  10.1 us (26%)
  waiting for transfers between devices  9.72 us (25%)
  local copies, waits for them, and re-layouts  1.87 us (5%)
    ppermute x16, starting transfers between devices, move(): return lax.ppermute(x, 'pb', pairs)  16.7 us
    ppermute x16, waiting for transfers between devices, move(): return lax.ppermute(x, 'pb', pairs)  9.72 us
    pallas_call x1, Pallas kernels, spectra_call(): pl.pallas_call(spectra_kernel, out_shape=[jax.ShapeDtypeStruct((rows, LAN...  5.35 us
    pallas_call x2, Pallas kernels, correlate_call(): pl.pallas_call(functools.partial(correlate_kernel, turn), out_shape=jax.S...  4.78 us
    unnamed x2, local copies, waits for them, and re-layouts  1.83 us
  transfers between devices with their start and end apart: 16, of which 8 were waited for; matrix products, arithmetic and copies ran while one was open for 5% of the time, Pallas kernels for 6%

profile of v4, /device:TPU:0, one launch (start us, length us, event | category | flops | bytes accessed | tf_op | source)
XLA Modules:
  0.0 38.5 jit_solution(13577409732105573178)
XLA Ops:
  0.0 5.4 %spectra.1 = (bf16[520,128]{1,0:T(8,128)(2,1)}, bf16[520,128]{1,0:T(8,128)(2,1)}) custom-call(s32[2]{0:T(128)} %mask_ref.1, f32[2,512,2048]{2,1,0:T(8,128)} %frames_ref.1, bf16[2,1024,256]{2,1,0:T(8,128)(2,1)} %constant.2.clone.table_ref), custom_call_target="tpu_custom_call" | custom-call | flops 2147483648 | bytes 8388608 | tf_op jit(solution)/shard_map/spectra/pallas_call | solution.py:99
  5.4 0.6 %collective-permute-start.4 = (bf16[520,128]{1,0:T(8,128)(2,1)}, bf16[520,128]{1,0:T(8,128)(2,1)S(1)}, u32[]{:S(2)}, u32[]{:S(2)}) collective-permute-start(bf16[520,128]{1,0:T(8,128)(2,1)} %get-tuple-element.7), channel_id=1, source_target_pairs={{0,1},{1,0},{2,3},{3,2},{4,5},{5,4},{6,7},{7,6},{8,9},{9,8},{10,11... | collective-permute-start | bytes 399368 | tf_op jit(solution)/shard_map/ppermute | solution.py:225
  5.9 0.1 collective-permute-start
  6.0 0.9 %constant_dynamic-update-slice_fusion.3 = bf16[1040,128]{1,0:T(8,128)(2,1)S(1)} fusion(bf16[520,128]{1,0:T(8,128)(2,1)} %get-tuple-element.8), kind=kLoop, calls=%fused_computation.3 | loop fusion | bytes 266240
  6.9 0.2 collective-permute-done.4
  7.1 3.0 %collective-permute-start.5 = (bf16[1040,128]{1,0:T(8,128)(2,1)S(1)}, bf16[1040,128]{1,0:T(8,128)(2,1)S(1)}, u32[]{:S(2)}, u32[]{:S(2)}) collective-permute-start(bf16[1040,128]{1,0:T(8,128)(2,1)S(1)} %constant_dynamic-update-slice_fusion.2.refs_0_), channel_id=1, source_target_pairs={{0,4},{1,3},{2,0},{3,7},{4,8},{5,1},{6,2},{7,11},{8,12},{9,5},{10,... | collective-permute-start | bytes 798728 | tf_op jit(solution)/shard_map/ppermute | solution.py:225
  10.1 0.9 %constant_dynamic-update-slice_fusion.1 = bf16[1040,128]{1,0:T(8,128)(2,1)S(1)} fusion(bf16[520,128]{1,0:T(8,128)(2,1)} %get-tuple-element.7), kind=kLoop, calls=%fused_computation.1 | loop fusion | bytes 266240
  11.0 0.0 collective-permute-done
  11.1 1.6 %collective-permute-start.1 = (bf16[1040,128]{1,0:T(8,128)(2,1)S(1)}, bf16[1040,128]{1,0:T(8,128)(2,1)S(1)}, u32[]{:S(2)}, u32[]{:S(2)}) collective-permute-start(bf16[1040,128]{1,0:T(8,128)(2,1)S(1)} %constant_dynamic-update-slice_fusion.refs_0_), channel_id=1, source_target_pairs={{0,4},{1,3},{2,0},{3,7},{4,8},{5,1},{6,2},{7,11},{8,12},{9,5},{10,... | collective-permute-start | bytes 798728 | tf_op jit(solution)/shard_map/ppermute | solution.py:225
  12.7 1.7 %collective-permute-done.5.refs_1_ = bf16[1040,128]{1,0:T(8,128)(2,1)S(1)} collective-permute-done((bf16[1040,128]{1,0:T(8,128)(2,1)S(1)}, bf16[1040,128]{1,0:T(8,128)(2,1)S(1)}, u32[]{:S(2)}, u32[]{:S(2)}) %collective-permute-start.5) | collective-permute-done | bytes 266272 | tf_op jit(solution)/shard_map/ppermute | solution.py:225
  14.4 2.1 %collective-permute-start.7 = (bf16[1040,128]{1,0:T(8,128)(2,1)S(1)}, bf16[1040,128]{1,0:T(8,128)(2,1)S(1)}, u32[]{:S(2)}, u32[]{:S(2)}) collective-permute-start(bf16[1040,128]{1,0:T(8,128)(2,1)S(1)} %collective-permute-done.5.refs_1_), channel_id=1, source_target_pairs={{0,4},{1,3},{2,0},{3,7},{4,8},{5,1},{6,2},{7,11},{8,12},{9,5},{10,... | collective-permute-start | bytes 798728 | tf_op jit(solution)/shard_map/ppermute | solution.py:225
  16.5 1.0 %collective-permute-done.1.refs_1_ = bf16[1040,128]{1,0:T(8,128)(2,1)S(1)} collective-permute-done((bf16[1040,128]{1,0:T(8,128)(2,1)S(1)}, bf16[1040,128]{1,0:T(8,128)(2,1)S(1)}, u32[]{:S(2)}, u32[]{:S(2)}) %collective-permute-start.1) | collective-permute-done | bytes 266272 | tf_op jit(solution)/shard_map/ppermute | solution.py:225
  17.5 1.8 %collective-permute-start.2 = (bf16[1040,128]{1,0:T(8,128)(2,1)S(1)}, bf16[1040,128]{1,0:T(8,128)(2,1)S(1)}, u32[]{:S(2)}, u32[]{:S(2)}) collective-permute-start(bf16[1040,128]{1,0:T(8,128)(2,1)S(1)} %collective-permute-done.1.refs_1_), channel_id=1, source_target_pairs={{0,4},{1,3},{2,0},{3,7},{4,8},{5,1},{6,2},{7,11},{8,12},{9,5},{10,... | collective-permute-start | bytes 798728 | tf_op jit(solution)/shard_map/ppermute | solution.py:225
  19.4 1.5 %collective-permute-done.7.refs_2_ = bf16[1040,128]{1,0:T(8,128)(2,1)S(1)} collective-permute-done((bf16[1040,128]{1,0:T(8,128)(2,1)S(1)}, bf16[1040,128]{1,0:T(8,128)(2,1)S(1)}, u32[]{:S(2)}, u32[]{:S(2)}) %collective-permute-start.7) | collective-permute-done | bytes 266272 | tf_op jit(solution)/shard_map/ppermute | solution.py:225
  20.9 2.1 %collective-permute-start.9 = (bf16[1040,128]{1,0:T(8,128)(2,1)S(1)}, bf16[1040,128]{1,0:T(8,128)(2,1)S(1)}, u32[]{:S(2)}, u32[]{:S(2)}) collective-permute-start(bf16[1040,128]{1,0:T(8,128)(2,1)S(1)} %collective-permute-done.7.refs_2_), channel_id=1, source_target_pairs={{0,4},{1,3},{2,0},{3,7},{4,8},{5,1},{6,2},{7,11},{8,12},{9,5},{10,... | collective-permute-start | bytes 798728 | tf_op jit(solution)/shard_map/ppermute | solution.py:225
  22.9 1.0 %collective-permute-done.2.refs_2_ = bf16[1040,128]{1,0:T(8,128)(2,1)S(1)} collective-permute-done((bf16[1040,128]{1,0:T(8,128)(2,1)S(1)}, bf16[1040,128]{1,0:T(8,128)(2,1)S(1)}, u32[]{:S(2)}, u32[]{:S(2)}) %collective-permute-start.2) | collective-permute-done | bytes 266272 | tf_op jit(solution)/shard_map/ppermute | solution.py:225
  24.0 1.8 %collective-permute-start.3 = (bf16[1040,128]{1,0:T(8,128)(2,1)S(1)}, bf16[1040,128]{1,0:T(8,128)(2,1)S(1)}, u32[]{:S(2)}, u32[]{:S(2)}) collective-permute-start(bf16[1040,128]{1,0:T(8,128)(2,1)S(1)} %collective-permute-done.2.refs_2_), channel_id=1, source_target_pairs={{0,4},{1,3},{2,0},{3,7},{4,8},{5,1},{6,2},{7,11},{8,12},{9,5},{10,... | collective-permute-start | bytes 798728 | tf_op jit(solution)/shard_map/ppermute | solution.py:225
  25.8 0.0 collective-permute-start.13
  25.8 0.5 %collective-permute-start.14 = (bf16[1040,128]{1,0:T(8,128)(2,1)S(1)}, bf16[1040,128]{1,0:T(8,128)(2,1)S(1)}, u32[]{:S(2)}, u32[]{:S(2)}) collective-permute-start(bf16[1040,128]{1,0:T(8,128)(2,1)S(1)} %collective-permute-done.2.refs_2_), channel_id=1, source_target_pairs={{0,1},{1,0},{2,3},{3,2},{4,5},{5,4},{6,7},{7,6},{8,9},{9,8},{10,11... | collective-permute-start | bytes 798728 | tf_op jit(solution)/shard_map/ppermute | solution.py:225
  26.3 1.0 %collective-permute-done.9.refs_3_ = bf16[1040,128]{1,0:T(8,128)(2,1)S(1)} collective-permute-done((bf16[1040,128]{1,0:T(8,128)(2,1)S(1)}, bf16[1040,128]{1,0:T(8,128)(2,1)S(1)}, u32[]{:S(2)}, u32[]{:S(2)}) %collective-permute-start.9) | collective-permute-done | bytes 266272 | tf_op jit(solution)/shard_map/ppermute | solution.py:225
  27.3 2.1 %collective-permute-start.11 = (bf16[1040,128]{1,0:T(8,128)(2,1)S(1)}, bf16[1040,128]{1,0:T(8,128)(2,1)S(1)}, u32[]{:S(2)}, u32[]{:S(2)}) collective-permute-start(bf16[1040,128]{1,0:T(8,128)(2,1)S(1)} %collective-permute-done.9.refs_3_), channel_id=1, source_target_pairs={{0,4},{1,3},{2,0},{3,7},{4,8},{5,1},{6,2},{7,11},{8,12},{9,5},{10,... | collective-permute-start | bytes 798728 | tf_op jit(solution)/shard_map/ppermute | solution.py:225
  29.4 1.0 %collective-permute-done.3.refs_3_ = bf16[1040,128]{1,0:T(8,128)(2,1)S(1)} collective-permute-done((bf16[1040,128]{1,0:T(8,128)(2,1)S(1)}, bf16[1040,128]{1,0:T(8,128)(2,1)S(1)}, u32[]{:S(2)}, u32[]{:S(2)}) %collective-permute-start.3) | collective-permute-done | bytes 266272 | tf_op jit(solution)/shard_map/ppermute | solution.py:225
  30.4 0.0 collective-permute-start.15
  30.4 0.5 %collective-permute-start.6 = (bf16[1040,128]{1,0:T(8,128)(2,1)S(1)}, bf16[1040,128]{1,0:T(8,128)(2,1)S(1)}, u32[]{:S(2)}, u32[]{:S(2)}) collective-permute-start(bf16[1040,128]{1,0:T(8,128)(2,1)S(1)} %collective-permute-done.5.refs_1_), channel_id=1, source_target_pairs={{0,1},{1,0},{2,3},{3,2},{4,5},{5,4},{6,7},{7,6},{8,9},{9,8},{10,11... | collective-permute-start | bytes 798728 | tf_op jit(solution)/shard_map/ppermute | solution.py:225
  30.9 0.0 collective-permute-done.13.refs_5_
  30.9 0.0 collective-permute-start.8
  30.9 0.0 collective-permute-done.14.refs_6_
  30.9 0.5 %collective-permute-start.10 = (bf16[1040,128]{1,0:T(8,128)(2,1)S(1)}, bf16[1040,128]{1,0:T(8,128)(2,1)S(1)}, u32[]{:S(2)}, u32[]{:S(2)}) collective-permute-start(bf16[1040,128]{1,0:T(8,128)(2,1)S(1)} %collective-permute-done.9.refs_3_), channel_id=1, source_target_pairs={{0,1},{1,0},{2,3},{3,2},{4,5},{5,4},{6,7},{7,6},{8,9},{9,8},{10,11... | collective-permute-start | bytes 798728 | tf_op jit(solution)/shard_map/ppermute | solution.py:225
  31.4 2.3 %collective-permute-done.11.refs_4_ = bf16[1040,128]{1,0:T(8,128)(2,1)S(1)} collective-permute-done((bf16[1040,128]{1,0:T(8,128)(2,1)S(1)}, bf16[1040,128]{1,0:T(8,128)(2,1)S(1)}, u32[]{:S(2)}, u32[]{:S(2)}) %collective-permute-start.11) | collective-permute-done | bytes 266272 | tf_op jit(solution)/shard_map/ppermute | solution.py:225
  33.7 0.0 collective-permute-start.12
  33.7 0.0 collective-permute-done.15.refs_7_
  33.7 2.4 %correlate.2.refs_8_ = f32[64,32,512]{2,1,0:T(8,128)} custom-call(bf16[1040,128]{1,0:T(8,128)(2,1)S(1)} %constant_dynamic-update-slice_fusion.2.refs_0_, bf16[1040,128]{1,0:T(8,128)(2,1)S(1)} %collective-permute-done.5.refs_1_, bf16[1040,128]{1,0:T(8,128)(2,1)S(1)} %collective-permute-done.7.refs_2_, bf16[1040,128]{1,0:T(8,128)(2,1)S(1)} %collective-permute-done.9.refs_3_, ...), custom_call_target="tpu_custom_call" | custom-call | flops 268435456 | bytes 2097152 | tf_op jit(solution)/shard_map/correlate/pallas_call | solution.py:196
  36.1 0.0 collective-permute-done.6.refs_4_
  36.1 0.0 collective-permute-done.8.refs_5_
  36.1 0.0 collective-permute-done.10.refs_6_
  36.1 0.0 collective-permute-done.12.refs_7_
  36.1 2.4 %correlate.3 = f32[64,32,512]{2,1,0:T(8,128)} custom-call(bf16[1040,128]{1,0:T(8,128)(2,1)S(1)} %constant_dynamic-update-slice_fusion.refs_0_, bf16[1040,128]{1,0:T(8,128)(2,1)S(1)} %collective-permute-done.1.refs_1_, bf16[1040,128]{1,0:T(8,128)(2,1)S(1)} %collective-permute-done.2.refs_2_, ...), custom_call_target="tpu_custom_call", output_to_operand_aliasing={{}: (8, {})} | custom-call | flops 268435456 | bytes 2097152 | tf_op jit(solution)/shard_map/correlate/pallas_call | solution.py:196
  (2 shorter events, 0.0 us)
Async XLA Ops:
  5.4 1.8 %collective-permute-start.4 = (bf16[520,128]{1,0:T(8,128)(2,1)}, bf16[520,128]{1,0:T(8,128)(2,1)S(1)}, u32[]{:S(2)}, u32[]{:S(2)}) collective-permute-start(bf16[520,128]{1,0:T(8,128)(2,1)} %get-tuple-element.7), channel_id=1, source_target_pairs={{0,1},{1,0},{2,3},{3,2},{4,5},{5,4},{6,7},{7,6},{8,9},{9,8},{10,11... | collective-permute-start | bytes 399368 | tf_op jit(solution)/shard_map/ppermute | solution.py:225
  5.9 5.1 %collective-permute-start = (bf16[520,128]{1,0:T(8,128)(2,1)}, bf16[520,128]{1,0:T(8,128)(2,1)S(1)}, u32[]{:S(2)}, u32[]{:S(2)}) collective-permute-start(bf16[520,128]{1,0:T(8,128)(2,1)} %get-tuple-element.8), channel_id=1, source_target_pairs={{0,1},{1,0},{2,3},{3,2},{4,5},{5,4},{6,7},{7,6},{8,9},{9,8},{10,11... | collective-permute-start | bytes 399368 | tf_op jit(solution)/shard_map/ppermute | solution.py:225
  7.1 7.3 %collective-permute-start.5 = (bf16[1040,128]{1,0:T(8,128)(2,1)S(1)}, bf16[1040,128]{1,0:T(8,128)(2,1)S(1)}, u32[]{:S(2)}, u32[]{:S(2)}) collective-permute-start(bf16[1040,128]{1,0:T(8,128)(2,1)S(1)} %constant_dynamic-update-slice_fusion.2.refs_0_), channel_id=1, source_target_pairs={{0,4},{1,3},{2,0},{3,7},{4,8},{5,1},{6,2},{7,11},{8,12},{9,5},{10,... | collective-permute-start | bytes 798728 | tf_op jit(solution)/shard_map/ppermute | solution.py:225
  11.1 6.5 %collective-permute-start.1 = (bf16[1040,128]{1,0:T(8,128)(2,1)S(1)}, bf16[1040,128]{1,0:T(8,128)(2,1)S(1)}, u32[]{:S(2)}, u32[]{:S(2)}) collective-permute-start(bf16[1040,128]{1,0:T(8,128)(2,1)S(1)} %constant_dynamic-update-slice_fusion.refs_0_), channel_id=1, source_target_pairs={{0,4},{1,3},{2,0},{3,7},{4,8},{5,1},{6,2},{7,11},{8,12},{9,5},{10,... | collective-permute-start | bytes 798728 | tf_op jit(solution)/shard_map/ppermute | solution.py:225
  14.4 6.4 %collective-permute-start.7 = (bf16[1040,128]{1,0:T(8,128)(2,1)S(1)}, bf16[1040,128]{1,0:T(8,128)(2,1)S(1)}, u32[]{:S(2)}, u32[]{:S(2)}) collective-permute-start(bf16[1040,128]{1,0:T(8,128)(2,1)S(1)} %collective-permute-done.5.refs_1_), channel_id=1, source_target_pairs={{0,4},{1,3},{2,0},{3,7},{4,8},{5,1},{6,2},{7,11},{8,12},{9,5},{10,... | collective-permute-start | bytes 798728 | tf_op jit(solution)/shard_map/ppermute | solution.py:225
  17.5 6.4 %collective-permute-start.2 = (bf16[1040,128]{1,0:T(8,128)(2,1)S(1)}, bf16[1040,128]{1,0:T(8,128)(2,1)S(1)}, u32[]{:S(2)}, u32[]{:S(2)}) collective-permute-start(bf16[1040,128]{1,0:T(8,128)(2,1)S(1)} %collective-permute-done.1.refs_1_), channel_id=1, source_target_pairs={{0,4},{1,3},{2,0},{3,7},{4,8},{5,1},{6,2},{7,11},{8,12},{9,5},{10,... | collective-permute-start | bytes 798728 | tf_op jit(solution)/shard_map/ppermute | solution.py:225
  20.9 6.4 %collective-permute-start.9 = (bf16[1040,128]{1,0:T(8,128)(2,1)S(1)}, bf16[1040,128]{1,0:T(8,128)(2,1)S(1)}, u32[]{:S(2)}, u32[]{:S(2)}) collective-permute-start(bf16[1040,128]{1,0:T(8,128)(2,1)S(1)} %collective-permute-done.7.refs_2_), channel_id=1, source_target_pairs={{0,4},{1,3},{2,0},{3,7},{4,8},{5,1},{6,2},{7,11},{8,12},{9,5},{10,... | collective-permute-start | bytes 798728 | tf_op jit(solution)/shard_map/ppermute | solution.py:225
  24.0 6.4 %collective-permute-start.3 = (bf16[1040,128]{1,0:T(8,128)(2,1)S(1)}, bf16[1040,128]{1,0:T(8,128)(2,1)S(1)}, u32[]{:S(2)}, u32[]{:S(2)}) collective-permute-start(bf16[1040,128]{1,0:T(8,128)(2,1)S(1)} %collective-permute-done.2.refs_2_), channel_id=1, source_target_pairs={{0,4},{1,3},{2,0},{3,7},{4,8},{5,1},{6,2},{7,11},{8,12},{9,5},{10,... | collective-permute-start | bytes 798728 | tf_op jit(solution)/shard_map/ppermute | solution.py:225
  25.8 5.1 %collective-permute-start.13 = (bf16[1040,128]{1,0:T(8,128)(2,1)S(1)}, bf16[1040,128]{1,0:T(8,128)(2,1)S(1)}, u32[]{:S(2)}, u32[]{:S(2)}) collective-permute-start(bf16[1040,128]{1,0:T(8,128)(2,1)S(1)} %collective-permute-done.1.refs_1_), channel_id=1, source_target_pairs={{0,1},{1,0},{2,3},{3,2},{4,5},{5,4},{6,7},{7,6},{8,9},{9,8},{10,11... | collective-permute-start | bytes 798728 | tf_op jit(solution)/shard_map/ppermute | solution.py:225
  25.8 5.1 %collective-permute-start.14 = (bf16[1040,128]{1,0:T(8,128)(2,1)S(1)}, bf16[1040,128]{1,0:T(8,128)(2,1)S(1)}, u32[]{:S(2)}, u32[]{:S(2)}) collective-permute-start(bf16[1040,128]{1,0:T(8,128)(2,1)S(1)} %collective-permute-done.2.refs_2_), channel_id=1, source_target_pairs={{0,1},{1,0},{2,3},{3,2},{4,5},{5,4},{6,7},{7,6},{8,9},{9,8},{10,11... | collective-permute-start | bytes 798728 | tf_op jit(solution)/shard_map/ppermute | solution.py:225
  27.3 6.4 %collective-permute-start.11 = (bf16[1040,128]{1,0:T(8,128)(2,1)S(1)}, bf16[1040,128]{1,0:T(8,128)(2,1)S(1)}, u32[]{:S(2)}, u32[]{:S(2)}) collective-permute-start(bf16[1040,128]{1,0:T(8,128)(2,1)S(1)} %collective-permute-done.9.refs_3_), channel_id=1, source_target_pairs={{0,4},{1,3},{2,0},{3,7},{4,8},{5,1},{6,2},{7,11},{8,12},{9,5},{10,... | collective-permute-start | bytes 798728 | tf_op jit(solution)/shard_map/ppermute | solution.py:225
  30.4 3.3 %collective-permute-start.15 = (bf16[1040,128]{1,0:T(8,128)(2,1)S(1)}, bf16[1040,128]{1,0:T(8,128)(2,1)S(1)}, u32[]{:S(2)}, u32[]{:S(2)}) collective-permute-start(bf16[1040,128]{1,0:T(8,128)(2,1)S(1)} %collective-permute-done.3.refs_3_), channel_id=1, source_target_pairs={{0,1},{1,0},{2,3},{3,2},{4,5},{5,4},{6,7},{7,6},{8,9},{9,8},{10,11... | collective-permute-start | bytes 798728 | tf_op jit(solution)/shard_map/ppermute | solution.py:225
  30.4 5.7 %collective-permute-start.6 = (bf16[1040,128]{1,0:T(8,128)(2,1)S(1)}, bf16[1040,128]{1,0:T(8,128)(2,1)S(1)}, u32[]{:S(2)}, u32[]{:S(2)}) collective-permute-start(bf16[1040,128]{1,0:T(8,128)(2,1)S(1)} %collective-permute-done.5.refs_1_), channel_id=1, source_target_pairs={{0,1},{1,0},{2,3},{3,2},{4,5},{5,4},{6,7},{7,6},{8,9},{9,8},{10,11... | collective-permute-start | bytes 798728 | tf_op jit(solution)/shard_map/ppermute | solution.py:225
  30.9 5.2 %collective-permute-start.8 = (bf16[1040,128]{1,0:T(8,128)(2,1)S(1)}, bf16[1040,128]{1,0:T(8,128)(2,1)S(1)}, u32[]{:S(2)}, u32[]{:S(2)}) collective-permute-start(bf16[1040,128]{1,0:T(8,128)(2,1)S(1)} %collective-permute-done.7.refs_2_), channel_id=1, source_target_pairs={{0,1},{1,0},{2,3},{3,2},{4,5},{5,4},{6,7},{7,6},{8,9},{9,8},{10,11... | collective-permute-start | bytes 798728 | tf_op jit(solution)/shard_map/ppermute | solution.py:225
  30.9 5.2 %collective-permute-start.10 = (bf16[1040,128]{1,0:T(8,128)(2,1)S(1)}, bf16[1040,128]{1,0:T(8,128)(2,1)S(1)}, u32[]{:S(2)}, u32[]{:S(2)}) collective-permute-start(bf16[1040,128]{1,0:T(8,128)(2,1)S(1)} %collective-permute-done.9.refs_3_), channel_id=1, source_target_pairs={{0,1},{1,0},{2,3},{3,2},{4,5},{5,4},{6,7},{7,6},{8,9},{9,8},{10,11... | collective-permute-start | bytes 798728 | tf_op jit(solution)/shard_map/ppermute | solution.py:225
  33.7 2.4 %collective-permute-start.12 = (bf16[1040,128]{1,0:T(8,128)(2,1)S(1)}, bf16[1040,128]{1,0:T(8,128)(2,1)S(1)}, u32[]{:S(2)}, u32[]{:S(2)}) collective-permute-start(bf16[1040,128]{1,0:T(8,128)(2,1)S(1)} %collective-permute-done.11.refs_4_), channel_id=1, source_target_pairs={{0,1},{1,0},{2,3},{3,2},{4,5},{5,4},{6,7},{7,6},{8,9},{9,8},{10,11... | collective-permute-start | bytes 798728 | tf_op jit(solution)/shard_map/ppermute | solution.py:225
